TPU v7x, 128 devices: a whole 4x4x4 slice. The times are simulated.
128 devices in a mesh: clip: 16 (over z, x), patch: 8 (over y, core).
Axes of the slice: x: 4, y: 4, z: 4, core: 2. Of those that a mesh axis runs over, the one named last changes fastest.
Arguments:
- pixels: bfloat16 [1024, 16, 64, 384], P(('clip', 'patch')), may hold values from -40 to 40
- destination: int32 [1024, 1], P(('clip', 'patch')), may hold values from 0 to 15; in each aligned block of 8 rows (0 to 7, 8 to 15, ...) at most 2 rows name the same one
- embed_weight: bfloat16 [384, 128], replicated, may hold values from -0.3125 to 0.3125
- embed_gain: float32 [128], replicated, may hold values from 0.5 to 2
- mixing_weight: bfloat16 [9, 384, 256], replicated, may hold values from -0.109375 to 0.109375
- mixing_gain: float32 [256], replicated, may hold values from 0.5 to 2
- project_weight: bfloat16 [256, 512], replicated, may hold values from -0.375 to 0.375
- project_gain: float32 [512], replicated, may hold values from 0.25 to 1.75
Outputs:
- latents: bfloat16 [4096, 8, 64, 512], P('clip', None, 'patch')
Inputs may be any that keep to these rules, and one draw needn't show every extreme that they name: `destination`: among the 8 clips of one owner device (aligned blocks of 8 rows) no tokenizer index occurs more than 2 times, and some index occurs exactly 2 times in some blocks.
All inputs are finite; a program needn't handle non-finite values.
Results may differ from a plain program's by a relative error of at most 0.0059.
Values may be sent and summed in bfloat16 or wider, within the bound.
A program may use at most 128 MiB of HBM per device.

v0:
```python
import functools

import jax
import jax.numpy as jnp
from jax import lax
from jax.experimental import pallas as pl
from jax.experimental.pallas import tpu as pltpu
from jax.sharding import PartitionSpec as P

GRID = 8
CAP = 2
OWN = 8
C1, C2, C3 = 128, 256, 512
GROUPS = 32
PAIR = 2
HI = lax.Precision.HIGHEST


def fold(rows, size):
    lanes = rows.shape[1]
    lane = lax.broadcasted_iota(jnp.int32, rows.shape, 1)
    step = 1
    while step < size:
        up = pltpu.roll(rows, lanes - step, 1)
        down = pltpu.roll(rows, step, 1)
        rows = rows + jnp.where((lane & step) == 0, up, down)
        step *= 2
    return rows


def group_sums(parts):
    channels = parts[0].shape[1]
    size = channels // GROUPS
    rows = []
    for part in parts:
        total = jnp.sum(part, axis=0, keepdims=True)
        rows += [total[:, i : i + 128] for i in range(0, channels, 128)]
    folded = fold(jnp.concatenate(rows, axis=0), size)
    each = channels // 128
    return [
        jnp.concatenate([folded[n * each + i : n * each + i + 1] for i in range(each)], axis=1)
        for n in range(len(parts))
    ]


def moments(parts):
    rows, channels = parts[0].shape
    inverse = 1.0 / (rows * (channels // GROUPS))
    means = [s * inverse for s in group_sums(parts)]
    squares = []
    for part, mean in zip(parts, means):
        centred = part - mean
        squares.append(centred * centred)
    scales = [lax.rsqrt(s * inverse + 1e-05) for s in group_sums(squares)]
    return means, scales


def silu(v):
    h = 0.5 * v
    return h + h * jnp.tanh(h)


def encode_pair(tubes, embed_w, embed_g, mixing_w, mixing_g, project_w, spread, act_refs):
    first = [jnp.dot(t, embed_w[...], preferred_element_type=jnp.float32) for t in tubes]
    means, scales = moments(first)
    for n in range(PAIR):
        act = silu((first[n] - means[n]) * (scales[n] * embed_g[...]))
        act = act.reshape(8, 2, GRID, GRID, C1)
        even, odd = act[:, 0], act[:, 1]
        place = lax.broadcasted_iota(jnp.int32, (8 * GRID * GRID, C1), 0) % GRID
        for j in range(3):
            for a, source in ((1, even), (2, odd)):
                flat = source.reshape(8 * GRID * GRID, C1)
                moved = source
                if j == 0:
                    moved = jnp.where(place == 0, 0.0, pltpu.roll(flat, 1, 0))
                elif j == 2:
                    moved = jnp.where(place == GRID - 1, 0.0, pltpu.roll(flat, 8 * GRID * GRID - 1, 0))
                moved = moved.reshape(8, GRID, GRID, C1)
                low = (j * 3 + a) * C1
                for y in range(GRID):
                    block = moved[:, y].reshape(64, C1)
                    spread[n, y, :, low : low + C1] = block.astype(jnp.bfloat16)
                    if a == 2:
                        prior = jnp.concatenate([jnp.zeros((GRID, C1), jnp.float32), block[:-GRID]], axis=0)
                        spread[n, y, :, low - 2 * C1 : low - C1] = prior.astype(jnp.bfloat16)
    second = []
    for n in range(PAIR):
        mid = jnp.dot(spread[n].reshape(512, 9 * C1), mixing_w[1], preferred_element_type=jnp.float32)
        low = jnp.dot(spread[n, 0:7].reshape(448, 9 * C1), mixing_w[0], preferred_element_type=jnp.float32)
        high = jnp.dot(spread[n, 1:8].reshape(448, 9 * C1), mixing_w[2], preferred_element_type=jnp.float32)
        none = jnp.zeros((64, C2), jnp.float32)
        second.append(
            mid + jnp.concatenate([none, low], axis=0) + jnp.concatenate([high, none], axis=0)
        )
    means, scales = moments(second)
    projected = []
    for n in range(PAIR):
        act = silu((second[n] - means[n]) * (scales[n] * mixing_g[...])).astype(jnp.bfloat16)
        act_refs[n][...] = act.reshape(GRID, 64, C2)
        projected.append(jnp.dot(act, project_w[...], preferred_element_type=jnp.float32))
    return moments(projected)


def pick_lanes(mean, scale):
    channel = lax.broadcasted_iota(jnp.int32, (C3, 128), 0)
    lane = lax.broadcasted_iota(jnp.int32, (C3, 128), 1)
    of_mean = ((channel == lane * 16) & (lane < 32)).astype(jnp.float32)
    of_scale = ((channel == (lane - 32) * 16) & (lane >= 32) & (lane < 64)).astype(jnp.float32)
    return jnp.dot(mean, of_mean, precision=HI, preferred_element_type=jnp.float32) + jnp.dot(
        scale, of_scale, precision=HI, preferred_element_type=jnp.float32
    )


def encode_kernel(
    slots, pixels, embed_w, embed_g, mixing_w, mixing_g, project_w, out, stats, spread, act, mean_s, scale_s, sems
):
    step = pl.program_id(0)
    steps = OWN // PAIR
    half = lax.rem(step, 2)

    def copies(at, buffer):
        return [
            pltpu.make_async_copy(
                act.at[buffer, n],
                out.at[slots[PAIR * at + n] // CAP, :, lax.rem(slots[PAIR * at + n], CAP)],
                sems.at[buffer, n],
            )
            for n in range(PAIR)
        ]

    @pl.when(step >= 2)
    def _():
        for copy in copies(step - 2, half):
            copy.wait()

    tubes = [pixels[n].reshape(1024, 384) for n in range(PAIR)]
    means, scales = encode_pair(
        tubes, embed_w, embed_g, mixing_w, mixing_g, project_w, spread, [act.at[half, n] for n in range(PAIR)]
    )
    for copy in copies(step, half):
        copy.start()
    for n in range(PAIR):
        mean_s[step, n : n + 1] = means[n]
        scale_s[step, n : n + 1] = scales[n]

    @pl.when(step == steps - 1)
    def _():
        mean = mean_s[:, 0:PAIR].reshape(OWN, C3)
        scale = scale_s[:, 0:PAIR].reshape(OWN, C3)
        stats[...] = pick_lanes(mean, scale)
        for at in (steps - 2, steps - 1):
            for copy in copies(at, at % 2):
                copy.wait()


def encode_call(slots, pixels, embed_w, embed_g, mixing_w, mixing_g, project_w):
    whole = lambda *shape: pl.BlockSpec(shape, lambda i, s: (0,) * len(shape), pipeline_mode=pl.Buffered(1))
    return pl.pallas_call(
        encode_kernel,
        grid_spec=pltpu.PrefetchScalarGridSpec(
            num_scalar_prefetch=1,
            grid=(OWN // PAIR,),
            in_specs=[
                pl.BlockSpec((PAIR, 16, 64, 384), lambda i, s: (i, 0, 0, 0)),
                whole(384, C1),
                whole(1, C1),
                whole(3, 9 * C1, C2),
                whole(1, C2),
                whole(C2, C3),
            ],
            out_specs=[pl.BlockSpec(memory_space=pl.ANY), whole(OWN, 128)],
            scratch_shapes=[
                pltpu.VMEM((PAIR, GRID, 64, 9 * C1), jnp.bfloat16),
                pltpu.VMEM((2, PAIR, GRID, 64, C2), jnp.bfloat16),
                pltpu.VMEM((OWN // PAIR, PAIR, C3), jnp.float32),
                pltpu.VMEM((OWN // PAIR, PAIR, C3), jnp.float32),
                pltpu.SemaphoreType.DMA((2, PAIR)),
            ],
        ),
        out_shape=[
            jax.ShapeDtypeStruct((16, GRID, CAP, 64, C2), jnp.bfloat16),
            jax.ShapeDtypeStruct((OWN, 128), jnp.float32),
        ],
        compiler_params=pltpu.CompilerParams(vmem_limit_bytes=60 * 2**20),
        name="encode",
    )(slots, pixels, embed_w, embed_g, mixing_w, mixing_g, project_w)


def decode_kernel(act, stats, weight, gain, out):
    group = lax.broadcasted_iota(jnp.int32, (128, C3), 1) // 16
    lane = lax.broadcasted_iota(jnp.int32, (128, C3), 0)
    st = stats[...]
    mean = jnp.dot(st, (lane == group).astype(jnp.float32), precision=HI, preferred_element_type=jnp.float32)
    scale = jnp.dot(st, (lane == group + 32).astype(jnp.float32), precision=HI, preferred_element_type=jnp.float32)
    scale = scale * gain[...]
    taken = jnp.broadcast_to(st[:, 64:65], mean.shape) > 0.5
    rows = act[...].reshape(-1, C2)
    values = jnp.dot(rows, weight[...], preferred_element_type=jnp.float32).reshape(-1, 64, C3)
    values = (values - mean[:, None, :]) * scale[:, None, :]
    out[...] = jnp.where(taken[:, None, :], values, 0.0).astype(jnp.bfloat16)


def decode_call(act, stats, weight, gain):
    return pl.pallas_call(
        decode_kernel,
        grid=(16,),
        in_specs=[
            pl.BlockSpec((8, None, CAP, 64, C2), lambda i: (i % 2, i // 2, 0, 0, 0)),
            pl.BlockSpec((16, 128), lambda i: (i, 0)),
            pl.BlockSpec((C2, C3), lambda i: (0, 0)),
            pl.BlockSpec((1, C3), lambda i: (0, 0)),
        ],
        out_specs=pl.BlockSpec((16, 64, C3), lambda i: (i, 0, 0)),
        out_shape=jax.ShapeDtypeStruct((256, 64, C3), jnp.bfloat16),
        compiler_params=pltpu.CompilerParams(vmem_limit_bytes=60 * 2**20),
        name="decode",
    )(act, stats, weight, gain)


def ranks_of(targets):
    order = jnp.arange(OWN, dtype=jnp.int32)
    same = targets[..., :, None] == targets[..., None, :]
    return jnp.sum((same & (order[:, None] > order[None, :])).astype(jnp.int32), axis=-1)


def on_device(
    pixels, destination, embed_weight, embed_gain, mixing_weight, mixing_gain, project_weight, project_gain
):
    targets = destination[:, 0]
    slots = targets * CAP + ranks_of(targets)
    outgoing, stats = encode_call(
        slots,
        pixels,
        embed_weight,
        embed_gain.reshape(1, C1),
        mixing_weight.reshape(3, 9 * C1, C2),
        mixing_gain.reshape(1, C2),
        project_weight,
    )
    arrived = lax.all_to_all(
        outgoing.reshape(128, CAP, 64, C2), ("clip", "patch"), split_axis=0, concat_axis=0, tiled=True
    )
    everyone = lax.all_gather(targets, ("clip", "patch"), axis=0)
    stats = lax.all_gather(stats, ("clip", "patch"), axis=0)
    rank = ranks_of(everyone)
    mine = everyone == lax.axis_index("clip")
    match = (mine[:, None, :] & (rank[:, None, :] == jnp.arange(CAP)[None, :, None])).astype(jnp.float32)
    stats = jnp.sum(match[..., None] * stats[:, None], axis=2)
    lane = jnp.arange(128)
    stats = jnp.where(lane == 64, jnp.sum(match, axis=2)[..., None], stats)
    stats = stats.reshape(16, GRID, CAP, 128).transpose(1, 0, 2, 3).reshape(256, 128)
    out = decode_call(
        arrived.reshape(16, GRID, CAP, 64, C2), stats, project_weight, project_gain.reshape(1, C3)
    )
    return out.reshape(256, 8, GRID, C3)


def solution(mesh):
    return jax.shard_map(
        on_device,
        mesh=mesh,
        in_specs=(P(("clip", "patch"), None, None, None), P(("clip", "patch"), None), P(), P(), P(), P(), P(), P()),
        out_specs=P("clip", None, "patch", None),
        check_vma=False,
    )
```

profile of v0, /device:TPU:1, one launch (start us, length us, event | category | flops | bytes accessed | tf_op | source)
XLA Modules:
  0.0 253.0 jit_solution(2304820914799589775)
XLA Ops:
  0.0 0.9 convert_reduce_fusion.1
  0.9 1.4 bitcast_dynamic-update-slice_fusion
  2.3 28.8 %encode.1 = (bf16[16,8,2,64,256]{4,3,2,1,0:T(8,128)(2,1)}, f32[8,128]{1,0:T(8,128)}) custom-call(s32[8]{0:T(128)} %get-tuple-element.10.slots, bf16[8,16,64,384]{3,2,1,0:T(8,128)(2,1)} %pixels.1, bf16[384,128]{1,0:T(8,128)(2,1)} %embed_w.1, f32[1,128]{1,0:T(1,128)} %bitcast.26, bf16[3,1152,256]{2,1,0:T(8,128)(2,1)} %bitcast.22, f32[1,256]{1,0:T(1,128)} %bitcast.25, ...), custom_call_target="tpu_custom_call" | custom-call | tf_op jit(solution)/shard_map/encode/pallas_call | solution.py:159
  31.1 0.0 copy-start
  31.1 12.0 %all-to-all-start = ((bf16[128,2,64,256]{3,2,1,0:T(8,128)(2,1)}), bf16[128,2,64,256]{3,2,1,0:T(8,128)(2,1)}, u32[]{:S(2)}, u32[]{:S(2)}) async-start(bf16[128,2,64,256]{3,2,1,0:T(8,128)(2,1)} %bitcast.20), calls=%async_computation | async-start | bytes 16777216 | tf_op jit(solution)/shard_map/all_to_all | solution.py:241
  43.1 155.7 %all-reduce = s32[1024]{0:T(1024)S(1)} all-reduce(s32[1024]{0:T(1024)S(1)} %get-tuple-element.9), channel_id=2, replica_groups=mesh['clip'=16,'patch'=8] {'clip','patch'}, use_global_device_ids=true, to_apply=%add | all-reduce | flops 1024 | bytes 8192
  198.8 0.1 reshape.60
  198.9 0.1 copy.10
  199.0 0.1 convert_reduce_fusion
  199.1 0.1 broadcast_in_dim.11
  199.2 0.1 copy.13
  199.4 0.0 copy-done
  199.4 34.7 %all-gather.1 = f32[1024,128]{1,0:T(8,128)S(1)} all-gather(f32[8,128]{1,0:T(8,128)S(1)} %copy-done), channel_id=3, replica_groups=mesh['clip'=16,'patch'=8] {'clip','patch'}, dimensions={0}, use_global_device_ids=true | all-gather | bytes 528384 | tf_op jit(solution)/shard_map/all_gather | solution.py:245
  234.1 0.4 multiply_reduce_fusion
  234.5 0.1 fusion
  234.6 0.8 copy.15
  235.4 0.0 all-to-all-done
  235.4 17.6 %decode.1 = bf16[256,64,512]{2,1,0:T(8,128)(2,1)} custom-call(bf16[16,8,2,64,256]{4,3,2,1,0:T(8,128)(2,1)} %bitcast.5.act, f32[256,128]{1,0:T(8,128)} %bitcast.23, bf16[256,512]{1,0:T(8,128)(2,1)} %weight.1, f32[1,512]{1,0:T(1,128)} %bitcast.24), custom_call_target="tpu_custom_call" | custom-call | tf_op jit(solution)/shard_map/decode/pallas_call | solution.py:205
  (7 shorter events, 0.1 us)
Async XLA Ops:
  31.1 168.3 %copy-start = (f32[8,128]{1,0:T(8,128)S(1)}, f32[8,128]{1,0:T(8,128)}, u32[]{:S(2)}) copy-start(f32[8,128]{1,0:T(8,128)} %get-tuple-element.8) | copy-start | bytes 12292
  31.1 204.3 %all-to-all-start = ((bf16[128,2,64,256]{3,2,1,0:T(8,128)(2,1)}), bf16[128,2,64,256]{3,2,1,0:T(8,128)(2,1)}, u32[]{:S(2)}, u32[]{:S(2)}) async-start(bf16[128,2,64,256]{3,2,1,0:T(8,128)(2,1)} %bitcast.20), calls=%async_computation | async-start | bytes 16777216 | tf_op jit(solution)/shard_map/all_to_all | solution.py:241
where the time goes:
time: 254 us; the launch traced here: 253 us
  blocking collectives  190 us (75%)
  Pallas kernels  46.5 us (18%)
  starting transfers between devices  12 us (5%)
  other arithmetic  2.95 us (1%)
    unnamed x1, blocking collectives  156 us
    all_gather x1, blocking collectives, on_device(): stats = lax.all_gather(stats, ('clip', 'patch'), axis=0)  34.7 us
    pallas_call x1, Pallas kernels, encode_call(): pl.pallas_call(encode_kernel, grid_spec=pltpu.PrefetchScalarGridSpec(num_...  28.8 us
    pallas_call x1, Pallas kernels, decode_call(): pl.pallas_call(decode_kernel, grid=(16,), in_specs=[pl.BlockSpec((8, None...  17.6 us
    all_to_all x1, starting transfers between devices, on_device(): lax.all_to_all(outgoing.reshape(128, CAP, 64, C2), ('clip', 'patch'), spl...  12 us
  transfers between devices with their start and end apart: 1, of which 0 were waited for; matrix products, arithmetic and copies ran while one was open for 1% of the time, Pallas kernels for 0%

commit v1 on v0

v1 whole, which is shorter than its diff:
```python
import functools

import jax
import jax.numpy as jnp
from jax import lax
from jax.experimental import pallas as pl
from jax.experimental.pallas import tpu as pltpu
from jax.sharding import PartitionSpec as P

GRID = 8
CAP = 2
OWN = 8
C1, C2, C3 = 128, 256, 512
GROUPS = 32
PAIR = 2
SIDE = 4
STEPS = OWN // PAIR
HI = lax.Precision.HIGHEST
MESH = pl.DeviceIdType.MESH


def fold(rows, size):
    lanes = rows.shape[1]
    lane = lax.broadcasted_iota(jnp.int32, rows.shape, 1)
    step = 1
    while step < size:
        up = pltpu.roll(rows, lanes - step, 1)
        down = pltpu.roll(rows, step, 1)
        rows = rows + jnp.where((lane & step) == 0, up, down)
        step *= 2
    return rows


def group_sums(parts):
    channels = parts[0].shape[1]
    size = channels // GROUPS
    rows = []
    for part in parts:
        total = jnp.sum(part, axis=0, keepdims=True)
        rows += [total[:, i : i + 128] for i in range(0, channels, 128)]
    folded = fold(jnp.concatenate(rows, axis=0), size)
    each = channels // 128
    return [
        jnp.concatenate([folded[n * each + i : n * each + i + 1] for i in range(each)], axis=1)
        for n in range(len(parts))
    ]


def moments(parts):
    rows, channels = parts[0].shape
    inverse = 1.0 / (rows * (channels // GROUPS))
    means = [s * inverse for s in group_sums(parts)]
    squares = []
    for part, mean in zip(parts, means):
        centred = part - mean
        squares.append(centred * centred)
    scales = [lax.rsqrt(s * inverse + 1e-05) for s in group_sums(squares)]
    return means, scales


def silu(v):
    h = 0.5 * v
    return h + h * jnp.tanh(h)


def encode_pair(tubes, embed_w, embed_g, mixing_w, mixing_g, project_w, spread, act, after):
    first = [jnp.dot(t, embed_w[...], preferred_element_type=jnp.float32) for t in tubes]
    means, scales = moments(first)
    for n in range(PAIR):
        wide = silu((first[n] - means[n]) * (scales[n] * embed_g[...]))
        wide = wide.reshape(8, 2, GRID, GRID, C1)
        even, odd = wide[:, 0], wide[:, 1]
        place = lax.broadcasted_iota(jnp.int32, (8 * GRID * GRID, C1), 0) % GRID
        for j in range(3):
            for a, source in ((1, even), (2, odd)):
                flat = source.reshape(8 * GRID * GRID, C1)
                moved = source
                if j == 0:
                    moved = jnp.where(place == 0, 0.0, pltpu.roll(flat, 1, 0))
                elif j == 2:
                    moved = jnp.where(place == GRID - 1, 0.0, pltpu.roll(flat, 8 * GRID * GRID - 1, 0))
                moved = moved.reshape(8, GRID, GRID, C1)
                low = (j * 3 + a) * C1
                for y in range(GRID):
                    block = moved[:, y].reshape(64, C1)
                    spread[n, y, :, low : low + C1] = block.astype(jnp.bfloat16)
                    if a == 2:
                        prior = jnp.concatenate([jnp.zeros((GRID, C1), jnp.float32), block[:-GRID]], axis=0)
                        spread[n, y, :, low - 2 * C1 : low - C1] = prior.astype(jnp.bfloat16)
    second = []
    for n in range(PAIR):
        mid = jnp.dot(spread[n].reshape(512, 9 * C1), mixing_w[1], preferred_element_type=jnp.float32)
        low = jnp.dot(spread[n, 0:7].reshape(448, 9 * C1), mixing_w[0], preferred_element_type=jnp.float32)
        high = jnp.dot(spread[n, 1:8].reshape(448, 9 * C1), mixing_w[2], preferred_element_type=jnp.float32)
        none = jnp.zeros((64, C2), jnp.float32)
        second.append(
            mid + jnp.concatenate([none, low], axis=0) + jnp.concatenate([high, none], axis=0)
        )
    means, scales = moments(second)
    acts = []
    for n in range(PAIR):
        acts.append(silu((second[n] - means[n]) * (scales[n] * mixing_g[...])).astype(jnp.bfloat16))
        act[:, n] = acts[n].reshape(GRID, 64, C2)
    after()
    return moments([jnp.dot(a, project_w[...], preferred_element_type=jnp.float32) for a in acts])


def pick_lanes(mean, scale):
    channel = lax.broadcasted_iota(jnp.int32, (C3, 128), 0)
    lane = lax.broadcasted_iota(jnp.int32, (C3, 128), 1)
    of_mean = ((channel == lane * 16) & (lane < 32)).astype(jnp.float32)
    of_scale = ((channel == (lane - 32) * 16) & (lane >= 32) & (lane < 64)).astype(jnp.float32)
    return jnp.dot(mean, of_mean, precision=HI, preferred_element_type=jnp.float32) + jnp.dot(
        scale, of_scale, precision=HI, preferred_element_type=jnp.float32
    )


class Place:
    def __init__(self):
        self.c, self.p = lax.axis_index("clip"), lax.axis_index("patch")
        self.z, self.x = self.c // SIDE, lax.rem(self.c, SIDE)

    def line(self, which):
        return self.z if which else self.x

    def beside(self, which, by):
        other = lax.rem(self.line(which) + by, SIDE)
        return (other * SIDE + self.x if which else self.z * SIDE + other, self.p), other

    def partner(self, by):
        other = lax.rem(self.p + by, GRID)
        return (self.c, other), other


def encode_kernel(
    order, pixels, embed_w, embed_g, mixing_w, mixing_g, project_w, extra,
    own, wide_x, wide_z, stats,
    tubes, spread, act, mean_s, scale_s, tile, pix_sem, send_y, recv_y, keep_y, send_g, recv_g, send_f, recv_f, send_s,
    recv_s, keep_s,
):
    me = Place()
    wide = (wide_x, wide_z)
    loads = [pltpu.make_async_copy(pixels.at[n], tubes.at[n], pix_sem.at[n]) for n in range(OWN)]
    for load in loads:
        load.start()
    barrier = pltpu.get_barrier_semaphore()
    for by in range(1, GRID):
        pl.semaphore_signal(barrier, inc=1, device_id=me.partner(by)[0], device_id_type=MESH)
    for which in range(2):
        for by in range(1, SIDE):
            pl.semaphore_signal(barrier, inc=1, device_id=me.beside(which, by)[0], device_id_type=MESH)
    pl.semaphore_wait(barrier, GRID - 1 + 2 * (SIDE - 1))
    for load in loads:
        load.wait()

    def remote(src, dst, send, recv, device):
        return pltpu.make_async_remote_copy(
            src_ref=src, dst_ref=dst, send_sem=send, recv_sem=recv, device_id=device, device_id_type=MESH
        )

    def across(m, by):
        device, other = me.partner(by)
        return remote(act.at[m, other], own.at[m, me.p], send_y.at[m, by], recv_y.at[m, me.p], device)

    def across_in(m, by):
        device, other = me.partner(by)
        return remote(act.at[m, other], own.at[m, other], send_y.at[m, by], recv_y.at[m, other], device)

    def kept(m):
        return pltpu.make_async_copy(act.at[m, me.p], own.at[m, me.p], keep_y.at[m])

    def gather(which, m, way):
        device, _ = me.beside(which, 1 if way == 0 else SIDE - 1)
        return remote(
            own.at[m, :, which], wide[which].at[me.line(which), m], send_g.at[which, m, way], recv_g.at[which, m, way], device
        )

    def gather_in(which, m, way):
        device, other = me.beside(which, SIDE - 1 if way == 0 else 1)
        return remote(
            own.at[m, :, which], wide[which].at[other, m], send_g.at[which, m, way], recv_g.at[which, m, way], device
        )

    def half(which, line, m, way):
        return wide[which].at[line, m, pl.ds(way * 4, 4)]

    def pass_on(which, m, way):
        _, origin = me.beside(which, SIDE - 1 if way == 0 else 1)
        device, _ = me.beside(which, 1 if way == 0 else SIDE - 1)
        part = half(which, origin, m, way)
        return remote(part, part, send_f.at[which, m, way], recv_f.at[which, m, way], device)

    def pass_on_in(which, m, way):
        device, origin = me.beside(which, 2)
        part = half(which, origin, m, way)
        return remote(part, part, send_f.at[which, m, way], recv_f.at[which, m, way], device)

    both = [(which, way) for which in range(2) for way in range(2)]

    def start_across(m):
        for by in range(1, GRID):
            across(m, by).start()
        kept(m).start()

    def start_gather(m):
        kept(m).wait()
        for by in range(1, GRID):
            across_in(m, by).wait_recv()
        for which, way in both:
            gather(which, m, way).start()

    def start_pass(m):
        for which, way in both:
            gather_in(which, m, way).wait_recv()
            pass_on(which, m, way).start()

    def encode(m):
        def after():
            @pl.when(m >= 1)
            def _():
                start_gather(m - 1)

            start_across(m)

            @pl.when(m >= 2)
            def _():
                start_pass(m - 2)

        values = [tubes[order[PAIR * m + n]].reshape(1024, 384) for n in range(PAIR)]
        means, scales = encode_pair(
            values, embed_w, embed_g, mixing_w, mixing_g, project_w, spread, act.at[m], after
        )
        for n in range(PAIR):
            mean_s[m, n : n + 1] = means[n]
            scale_s[m, n : n + 1] = scales[n]

    def stat_y(by, incoming):
        device, other = me.partner(by)
        at = other if incoming else me.p
        return remote(tile, stats.at[me.c, at], send_s.at[by], recv_s.at[0, at], device)

    def stat_x(by, incoming):
        device, other = me.beside(0, by)
        row = stats.at[me.z * SIDE + (other if incoming else me.x)]
        return remote(stats.at[me.c], row, send_s.at[GRID + by], recv_s.at[1, other if incoming else me.x], device)

    def stat_z(by, incoming):
        device, other = me.beside(1, by)
        mine = stats.at[pl.ds(me.z * SIDE, SIDE)]
        rows = stats.at[pl.ds((other if incoming else me.z) * SIDE, SIDE)]
        return remote(mine, rows, send_s.at[GRID + SIDE + by], recv_s.at[2, other if incoming else me.z], device)

    def loop(m, carry):
        encode(m)
        return carry

    lax.fori_loop(0, STEPS, loop, 0)
    mean = mean_s[...].reshape(OWN, C3)
    scale = scale_s[...].reshape(OWN, C3)
    tile[...] = pick_lanes(mean, scale) + extra[...]
    for by in range(1, GRID):
        stat_y(by, False).start()
    keep = pltpu.make_async_copy(tile, stats.at[me.c, me.p], keep_s.at[0])
    keep.start()
    start_gather(STEPS - 1)
    start_pass(STEPS - 2)
    keep.wait()
    for by in range(1, GRID):
        stat_y(by, True).wait_recv()
    for by in range(1, SIDE):
        stat_x(by, False).start()
    for by in range(1, SIDE):
        stat_x(by, True).wait_recv()
    for by in range(1, SIDE):
        stat_z(by, False).start()
    start_pass(STEPS - 1)

    def drain(m, carry):
        for by in range(1, GRID):
            across(m, by).wait_send()
        for which, way in both:
            gather(which, m, way).wait_send()
            pass_on_in(which, m, way).wait_recv()
            pass_on(which, m, way).wait_send()
        return carry

    lax.fori_loop(0, STEPS, drain, 0)
    for by in range(1, SIDE):
        stat_z(by, True).wait_recv()
    for by in range(1, GRID):
        stat_y(by, False).wait_send()
    for by in range(1, SIDE):
        stat_x(by, False).wait_send()
        stat_z(by, False).wait_send()


def encode_call(order, pixels, embed_w, embed_g, mixing_w, mixing_g, project_w, extra):
    anywhere = pl.BlockSpec(memory_space=pl.ANY)
    inside = pl.BlockSpec(memory_space=pltpu.VMEM)
    dma = pltpu.SemaphoreType.DMA
    return pl.pallas_call(
        encode_kernel,
        in_specs=[pl.BlockSpec(memory_space=pltpu.SMEM), anywhere] + [inside] * 6,
        out_specs=[anywhere] * 4,
        out_shape=[
            jax.ShapeDtypeStruct((STEPS, GRID, PAIR, 64, C2), jnp.bfloat16),
            jax.ShapeDtypeStruct((SIDE, STEPS, GRID, 64, C2), jnp.bfloat16),
            jax.ShapeDtypeStruct((SIDE, STEPS, GRID, 64, C2), jnp.bfloat16),
            jax.ShapeDtypeStruct((SIDE * SIDE, GRID, OWN, 128), jnp.float32),
        ],
        scratch_shapes=[
            pltpu.VMEM((OWN, 16, 64, 384), jnp.bfloat16),
            pltpu.VMEM((PAIR, GRID, 64, 9 * C1), jnp.bfloat16),
            pltpu.VMEM((STEPS, GRID, PAIR, 64, C2), jnp.bfloat16),
            pltpu.VMEM((STEPS, PAIR, C3), jnp.float32),
            pltpu.VMEM((STEPS, PAIR, C3), jnp.float32),
            pltpu.VMEM((OWN, 128), jnp.float32),
            dma((OWN,)),
            dma((STEPS, GRID)),
            dma((STEPS, GRID)),
            dma((STEPS,)),
            dma((2, STEPS, 2)),
            dma((2, STEPS, 2)),
            dma((2, STEPS, 2)),
            dma((2, STEPS, 2)),
            dma((GRID + 2 * SIDE,)),
            dma((3, GRID)),
            dma((1,)),
        ],
        compiler_params=pltpu.CompilerParams(vmem_limit_bytes=60 * 2**20, collective_id=0, has_side_effects=True),
        name="encode",
    )(order, pixels, embed_w, embed_g, mixing_w, mixing_g, project_w, extra)


def route_kernel(table, own, wide_x, wide_z, out, held_x, held_z, packed, load_sem, send_sem, recv_sem, keep_sem):
    me = Place()
    wide = (wide_x, wide_z)
    held = (held_x, held_z)

    def loads(which):
        copies = [
            pltpu.make_async_copy(own.at[:, :, which], held[which].at[me.line(which)], load_sem.at[which, 0])
        ]
        for by in range(1, SIDE):
            _, other = me.beside(which, by)
            copies.append(
                pltpu.make_async_copy(wide[which].at[other], held[which].at[other], load_sem.at[which, by])
            )
        return copies

    for which in range(2):
        for copy in loads(which):
            copy.start()
    barrier = pltpu.get_barrier_semaphore()
    for which in range(2):
        for by in range(1, SIDE):
            pl.semaphore_signal(barrier, inc=1, device_id=me.beside(which, by)[0], device_id_type=MESH)
    pl.semaphore_wait(barrier, 2 * (SIDE - 1))

    def target(which, line):
        return out.at[1, :, line] if which else out.at[0, line]

    def send(which, by, incoming):
        device, other = me.beside(1 - which, by)
        line = me.line(1 - which)
        return pltpu.make_async_remote_copy(
            src_ref=packed.at[which, other],
            dst_ref=target(which, other if incoming else line),
            send_sem=send_sem.at[which, by],
            recv_sem=recv_sem.at[which, other if incoming else line],
            device_id=device,
            device_id_type=MESH,
        )

    def keep(which):
        line = me.line(1 - which)
        return pltpu.make_async_copy(packed.at[which, line], target(which, line), keep_sem.at[which])

    def pack(which, other):
        def one(i, carry):
            s, p = i // GRID, lax.rem(i, GRID)
            m = table[(which * SIDE + other) * SIDE * GRID + i]
            packed[which, other, s, p] = held[which][s, m, p]
            return carry

        lax.fori_loop(0, SIDE * GRID, one, 0)

    for by in (2, 1, 3, 0):
        for which in range(2):
            if by == 2:
                for copy in loads(which):
                    copy.wait()
            _, other = me.beside(1 - which, by)
            pack(which, other)
            if by:
                send(which, by, False).start()
            else:
                keep(which).start()
    for which in range(2):
        keep(which).wait()
        for by in range(1, SIDE):
            send(which, by, True).wait_recv()
            send(which, by, False).wait_send()


def route_call(table, own, wide_x, wide_z):
    anywhere = pl.BlockSpec(memory_space=pl.ANY)
    dma = pltpu.SemaphoreType.DMA
    return pl.pallas_call(
        route_kernel,
        in_specs=[pl.BlockSpec(memory_space=pltpu.SMEM)] + [anywhere] * 3,
        out_specs=anywhere,
        out_shape=jax.ShapeDtypeStruct((2, SIDE, SIDE, GRID, 64, C2), jnp.bfloat16),
        scratch_shapes=[
            pltpu.VMEM((SIDE, STEPS, GRID, 64, C2), jnp.bfloat16),
            pltpu.VMEM((SIDE, STEPS, GRID, 64, C2), jnp.bfloat16),
            pltpu.VMEM((2, SIDE, SIDE, GRID, 64, C2), jnp.bfloat16),
            dma((2, SIDE)),
            dma((2, SIDE)),
            dma((2, SIDE)),
            dma((2,)),
        ],
        compiler_params=pltpu.CompilerParams(vmem_limit_bytes=60 * 2**20, collective_id=1, has_side_effects=True),
        name="route",
    )(table, own, wide_x, wide_z)


def decode_kernel(parity, act, stats, weight, gain, out, rows):
    step = pl.program_id(0)
    group = lax.broadcasted_iota(jnp.int32, (128, C3), 1) // 16
    lane = lax.broadcasted_iota(jnp.int32, (128, C3), 0)
    st = stats[...]
    mean = jnp.dot(st, (lane == group).astype(jnp.float32), precision=HI, preferred_element_type=jnp.float32)
    scale = jnp.dot(st, (lane == group + 32).astype(jnp.float32), precision=HI, preferred_element_type=jnp.float32)
    scale = scale * gain[...]
    taken = jnp.broadcast_to(st[:, 64:65], mean.shape) > 0.5
    for i in range(8):
        first = parity[step * 8 + i]
        rows[2 * i] = act[first, i]
        rows[2 * i + 1] = act[1 - first, i]
    values = jnp.dot(rows[...].reshape(-1, C2), weight[...], preferred_element_type=jnp.float32).reshape(-1, 64, C3)
    values = (values - mean[:, None, :]) * scale[:, None, :]
    out[...] = jnp.where(taken[:, None, :], values, 0.0).astype(jnp.bfloat16)


def decode_call(parity, act, stats, weight, gain):
    return pl.pallas_call(
        decode_kernel,
        grid_spec=pltpu.PrefetchScalarGridSpec(
            num_scalar_prefetch=1,
            grid=(16,),
            in_specs=[
                pl.BlockSpec((2, 8, None, 64, C2), lambda i, s: (0, i % 2, i // 2, 0, 0)),
                pl.BlockSpec((16, 128), lambda i, s: (i, 0)),
                pl.BlockSpec((C2, C3), lambda i, s: (0, 0)),
                pl.BlockSpec((1, C3), lambda i, s: (0, 0)),
            ],
            out_specs=pl.BlockSpec((16, 64, C3), lambda i, s: (i, 0, 0)),
            scratch_shapes=[pltpu.VMEM((16, 64, C2), jnp.bfloat16)],
        ),
        out_shape=jax.ShapeDtypeStruct((256, 64, C3), jnp.bfloat16),
        compiler_params=pltpu.CompilerParams(vmem_limit_bytes=60 * 2**20),
        name="decode",
    )(parity, act, stats, weight, gain)


def on_device(
    pixels, destination, embed_weight, embed_gain, mixing_weight, mixing_gain, project_weight, project_gain
):
    targets = destination[:, 0]
    here = jnp.arange(OWN, dtype=jnp.int32)
    ahead = (targets[None, :] < targets[:, None]) | (
        (targets[None, :] == targets[:, None]) & (here[None, :] < here[:, None])
    )
    sorted_at = jnp.sum(ahead.astype(jnp.int32), axis=1)
    hits = sorted_at[None, :] == here[:, None]
    order = jnp.sum(jnp.where(hits, here[None, :], 0), axis=1)
    in_order = jnp.sum(jnp.where(hits, targets[None, :], 0), axis=1)
    lane = jnp.arange(128)
    extra = jnp.where(lane[None, :] == 64, in_order[:, None].astype(jnp.float32), 0.0)
    own, wide_x, wide_z, stats = encode_call(
        order,
        pixels,
        embed_weight,
        embed_gain.reshape(1, C1),
        mixing_weight.reshape(3, 9 * C1, C2),
        mixing_gain.reshape(1, C2),
        project_weight,
        extra,
    )
    c = lax.axis_index("clip")
    z, x = c // SIDE, c % SIDE
    named = jnp.round(stats[:, :, :, 64]).astype(jnp.int32)
    grid = named.reshape(SIDE, SIDE, GRID, STEPS, PAIR)
    steps = jnp.arange(STEPS)
    lines = jnp.arange(SIDE)
    row = lax.dynamic_index_in_dim(grid, z, 0, keepdims=False)[..., 0]
    column = lax.dynamic_index_in_dim(grid, x, 1, keepdims=False)[..., 1]
    to_z = jnp.sum(jnp.where(row[None] == (lines * SIDE + x)[:, None, None, None], steps, 0), axis=-1)
    to_x = jnp.sum(jnp.where(column[None] == (z * SIDE + lines)[:, None, None, None], steps, 0), axis=-1)
    table = jnp.concatenate([to_z.reshape(-1), to_x.reshape(-1)])
    arrived = route_call(table, own, wide_x, wide_z)
    named = named.transpose(1, 0, 2)
    again = jnp.concatenate([jnp.zeros((GRID, 16, 1), bool), named[:, :, 1:] == named[:, :, :-1]], axis=2)
    mine = named == c
    match = jnp.stack([mine & ~again, mine & again], axis=2)
    parity = jnp.sum(jnp.where(match[:, :, 0], here % 2, 0), axis=-1).reshape(128)
    chosen = jnp.sum(jnp.where(match[..., None], stats.transpose(1, 0, 2, 3)[:, :, None], 0.0), axis=3)
    chosen = jnp.where(lane == 64, jnp.any(match, axis=3)[..., None].astype(jnp.float32), chosen)
    out = decode_call(
        parity,
        arrived.reshape(2, 16, GRID, 64, C2),
        chosen.reshape(256, 128),
        project_weight,
        project_gain.reshape(1, C3),
    )
    return out.reshape(256, 8, GRID, C3)


def solution(mesh):
    return jax.shard_map(
        on_device,
        mesh=mesh,
        in_specs=(P(("clip", "patch"), None, None, None), P(("clip", "patch"), None), P(), P(), P(), P(), P(), P()),
        out_specs=P("clip", None, "patch", None),
        check_vma=False,
    )
```

time: 254 us -> 153 us (0.60)
  blocking collectives: 190 us -> 0 us
  Pallas kernels: 46.5 us -> 143 us
  starting transfers between devices: 12 us -> 0 us
  other arithmetic: 2.95 us -> 6.44 us
    unnamed x1 -> x0, blocking collectives: 156 us -> none
    pallas_call x2 -> x3, Pallas kernels: 46.5 us -> 143 us  [the longest x1 72.7 us: encode_call(): pl.pallas_call(encode_kernel, in_specs=[pl.BlockSpec(memory_space=pltpu.S...]
    all_gather x1 -> x0, blocking collectives: 34.7 us -> none  [on_device(): stats = lax.all_gather(stats, ('clip', 'patch'), axis=0)]
    all_to_all x1 -> x0, starting transfers between devices: 12 us -> none  [on_device(): lax.all_to_all(outgoing.reshape(128, CAP, 64, C2), ('clip', 'patch'), spl...]
  transfers between devices with their start and end apart: 1 -> 0, of which waited for: 0 -> 0; matrix products, arithmetic and copies ran while one was open for 1% -> 0% of each run, Pallas kernels for 0% -> 0%
where the time goes in v1:
time: 153 us; the launch traced here: 152 us
  Pallas kernels  143 us (93%)
  other arithmetic  6.44 us (4%)
  local copies, waits for them, and re-layouts  2.63 us (2%)
    pallas_call x1, Pallas kernels, encode_call(): pl.pallas_call(encode_kernel, in_specs=[pl.BlockSpec(memory_space=pltpu.S...  72.7 us
    pallas_call x1, Pallas kernels, route_call(): pl.pallas_call(route_kernel, in_specs=[pl.BlockSpec(memory_space=pltpu.SM...  52 us
    pallas_call x1, Pallas kernels, decode_call(): pl.pallas_call(decode_kernel, grid_spec=pltpu.PrefetchScalarGridSpec(num_...  18.3 us

profile of v1, /device:TPU:1, one launch (start us, length us, event | category | flops | bytes accessed | tf_op | source)
XLA Modules:
  0.0 152.3 jit_solution(11746828887346249054)
XLA Ops:
  0.0 0.9 convert_reduce_fusion
  0.9 1.4 select_reduce_fusion.4
  2.3 0.7 broadcast_select_fusion.1.extra
  3.0 72.7 %encode.1 = (bf16[4,8,2,64,256]{4,3,2,1,0:T(8,128)(2,1)}, bf16[4,4,8,64,256]{4,3,2,1,0:T(8,128)(2,1)}, bf16[4,4,8,64,256]{4,3,2,1,0:T(8,128)(2,1)}, f32[16,8,8,128]{3,2,1,0:T(8,128)}) custom-call(s32[8]{0:T(128)} %get-tuple-element.14.order, bf16[8,16,64,384]{3,2,1,0:T(8,128)(2,1)} %pixels.1, bf16[384,128]{1,0:T(8,128)(2,1)} %embed_w.1, f32[1,128]{1,0:T(1,128)} %bitcast.42, ...), custom_call_target="tpu_custom_call" | custom-call | tf_op jit(solution)/shard_map/encode/pallas_call | solution.py:301
  75.7 1.2 round-nearest-even_convert_fusion
  76.9 0.5 copy.45
  77.4 0.8 copy.46
  78.3 0.1 select_reduce_fusion.3
  78.4 0.7 reshape.71.parity
  79.2 0.1 select_reduce_fusion.2
  79.3 0.1 reshape.72
  79.4 0.1 select_reduce_fusion.1
  79.5 0.1 reshape.73
  79.6 0.6 pad_add_fusion.1.table
  80.2 0.0 copy-start
  80.2 52.0 %route.1 = bf16[2,4,4,8,64,256]{5,4,3,2,1,0:T(8,128)(2,1)} custom-call(s32[256]{0:T(256)} %pad_add_fusion.1.table, bf16[4,8,2,64,256]{4,3,2,1,0:T(8,128)(2,1)} %get-tuple-element.10.own, bf16[4,4,8,64,256]{4,3,2,1,0:T(8,128)(2,1)} %get-tuple-element.11.wide_x, bf16[4,4,8,64,256]{4,3,2,1,0:T(8,128)(2,1)} %get-tuple-element.12.wide_z), custom_call_target="tpu_custom_call" | custom-call | tf_op jit(solution)/shard_map/route/pallas_call | solution.py:409
  132.2 0.1 copy.49
  132.3 0.1 reshape.77
  132.5 0.2 copy.50
  132.6 0.0 copy-done
  132.7 0.5 select_reduce_fusion
  133.2 0.8 broadcast_select_fusion.stats
  133.9 18.3 %decode.1 = bf16[256,64,512]{2,1,0:T(8,128)(2,1)} custom-call(s32[128]{0:T(128)} %reshape.71.parity, bf16[2,16,8,64,256]{4,3,2,1,0:T(8,128)(2,1)} %bitcast.32, f32[256,128]{1,0:T(8,128)} %broadcast_select_fusion.stats, bf16[256,512]{1,0:T(8,128)(2,1)} %weight.1, f32[1,512]{1,0:T(1,128)} %bitcast.40), custom_call_target="tpu_custom_call" | custom-call | tf_op jit(solution)/shard_map/decode/pallas_call | solution.py:447
  (16 shorter events, 0.2 us)
Async XLA Ops:
  80.2 52.5 %copy-start = (f32[16,8,8,128]{3,2,1,0:T(8,128)S(1)}, f32[16,8,8,128]{3,2,1,0:T(8,128)}, u32[]{:S(2)}) copy-start(f32[16,8,8,128]{3,2,1,0:T(8,128)} %get-tuple-element.9) | copy-start | bytes 1572868

commit v2 on v1

v2 whole, which is shorter than its diff:
```python
import functools

import jax
import jax.numpy as jnp
from jax import lax
from jax.experimental import pallas as pl
from jax.experimental.pallas import tpu as pltpu
from jax.sharding import PartitionSpec as P

GRID = 8
CAP = 2
OWN = 8
C1, C2, C3 = 128, 256, 512
GROUPS = 32
PAIR = 2
SIDE = 4
STEPS = OWN // PAIR
HI = lax.Precision.HIGHEST
MESH = pl.DeviceIdType.MESH


def fold(rows, size):
    lanes = rows.shape[1]
    lane = lax.broadcasted_iota(jnp.int32, rows.shape, 1)
    step = 1
    while step < size:
        up = pltpu.roll(rows, lanes - step, 1)
        down = pltpu.roll(rows, step, 1)
        rows = rows + jnp.where((lane & step) == 0, up, down)
        step *= 2
    return rows


def group_sums(parts):
    channels = parts[0].shape[1]
    size = channels // GROUPS
    rows = []
    for part in parts:
        total = jnp.sum(part, axis=0, keepdims=True)
        rows += [total[:, i : i + 128] for i in range(0, channels, 128)]
    folded = fold(jnp.concatenate(rows, axis=0), size)
    each = channels // 128
    return [
        jnp.concatenate([folded[n * each + i : n * each + i + 1] for i in range(each)], axis=1)
        for n in range(len(parts))
    ]


def moments(parts):
    rows, channels = parts[0].shape
    inverse = 1.0 / (rows * (channels // GROUPS))
    means = [s * inverse for s in group_sums(parts)]
    squares = []
    for part, mean in zip(parts, means):
        centred = part - mean
        squares.append(centred * centred)
    scales = [lax.rsqrt(s * inverse + 1e-05) for s in group_sums(squares)]
    return means, scales


def silu(v):
    h = 0.5 * v
    return h + h * jnp.tanh(h)


def encode_pair(tubes, embed_w, embed_g, mixing_w, mixing_g, project_w, spread, act, after):
    first = [jnp.dot(t, embed_w[...], preferred_element_type=jnp.float32) for t in tubes]
    means, scales = moments(first)
    for n in range(PAIR):
        wide = silu((first[n] - means[n]) * (scales[n] * embed_g[...]))
        wide = wide.reshape(8, 2, GRID, GRID, C1)
        even, odd = wide[:, 0], wide[:, 1]
        place = lax.broadcasted_iota(jnp.int32, (8 * GRID * GRID, C1), 0) % GRID
        for j in range(3):
            for a, source in ((1, even), (2, odd)):
                flat = source.reshape(8 * GRID * GRID, C1)
                moved = source
                if j == 0:
                    moved = jnp.where(place == 0, 0.0, pltpu.roll(flat, 1, 0))
                elif j == 2:
                    moved = jnp.where(place == GRID - 1, 0.0, pltpu.roll(flat, 8 * GRID * GRID - 1, 0))
                moved = moved.reshape(8, GRID, GRID, C1)
                low = (j * 3 + a) * C1
                for y in range(GRID):
                    block = moved[:, y].reshape(64, C1)
                    spread[n, y, :, low : low + C1] = block.astype(jnp.bfloat16)
                    if a == 2:
                        prior = jnp.concatenate([jnp.zeros((GRID, C1), jnp.float32), block[:-GRID]], axis=0)
                        spread[n, y, :, low - 2 * C1 : low - C1] = prior.astype(jnp.bfloat16)
    second = []
    for n in range(PAIR):
        mid = jnp.dot(spread[n].reshape(512, 9 * C1), mixing_w[1], preferred_element_type=jnp.float32)
        low = jnp.dot(spread[n, 0:7].reshape(448, 9 * C1), mixing_w[0], preferred_element_type=jnp.float32)
        high = jnp.dot(spread[n, 1:8].reshape(448, 9 * C1), mixing_w[2], preferred_element_type=jnp.float32)
        none = jnp.zeros((64, C2), jnp.float32)
        second.append(
            mid + jnp.concatenate([none, low], axis=0) + jnp.concatenate([high, none], axis=0)
        )
    means, scales = moments(second)
    acts = []
    for n in range(PAIR):
        acts.append(silu((second[n] - means[n]) * (scales[n] * mixing_g[...])).astype(jnp.bfloat16))
        act[:, n] = acts[n].reshape(GRID, 64, C2)
    after()
    return moments([jnp.dot(a, project_w[...], preferred_element_type=jnp.float32) for a in acts])


def pick_lanes(mean, scale):
    channel = lax.broadcasted_iota(jnp.int32, (C3, 128), 0)
    lane = lax.broadcasted_iota(jnp.int32, (C3, 128), 1)
    of_mean = ((channel == lane * 16) & (lane < 32)).astype(jnp.float32)
    of_scale = ((channel == (lane - 32) * 16) & (lane >= 32) & (lane < 64)).astype(jnp.float32)
    return jnp.dot(mean, of_mean, precision=HI, preferred_element_type=jnp.float32) + jnp.dot(
        scale, of_scale, precision=HI, preferred_element_type=jnp.float32
    )


class Place:
    def __init__(self):
        self.c, self.p = lax.axis_index("clip"), lax.axis_index("patch")
        self.z, self.x = self.c // SIDE, lax.rem(self.c, SIDE)

    def line(self, which):
        return self.z if which else self.x

    def beside(self, which, by):
        other = lax.rem(self.line(which) + by, SIDE)
        return (other * SIDE + self.x if which else self.z * SIDE + other, self.p), other

    def partner(self, by):
        other = lax.rem(self.p + by, GRID)
        return (self.c, other), other


def exchange_kernel(
    dest, pixels, embed_w, embed_g, mixing_w, mixing_g, project_w,
    arrived, marks, parity, names,
    tubes, spread, act, own, wide_x, wide_z, packed, mean_s, scale_s, tile, tiles, lines, pack_s, name_row, name_s, order,
    pix_sem, send_n, recv_n, keep_n, send_y, recv_y, keep_y, send_g, recv_g, keep_g, send_f, recv_f, send_s, recv_s, keep_s,
    send_l, recv_l, keep_l, send_r, recv_r, keep_r, send_q, recv_q, keep_q,
):
    me = Place()
    wide = (wide_x, wide_z)
    loads = [pltpu.make_async_copy(pixels.at[n], tubes.at[n], pix_sem.at[n]) for n in range(OWN)]
    for load in loads:
        load.start()
    barrier = pltpu.get_barrier_semaphore()
    for by in range(1, GRID):
        pl.semaphore_signal(barrier, inc=1, device_id=me.partner(by)[0], device_id_type=MESH)
    for which in range(2):
        for by in range(1, SIDE):
            pl.semaphore_signal(barrier, inc=1, device_id=me.beside(which, by)[0], device_id_type=MESH)

    d = [dest[k, 0] for k in range(OWN)]
    at = []
    for k in range(OWN):
        ahead = [((d[j] <= d[k]) if j < k else (d[j] < d[k])).astype(jnp.int32) for j in range(OWN) if j != k]
        at.append(functools.reduce(lambda a, b: a + b, ahead))
    lane = lax.broadcasted_iota(jnp.int32, (1, 128), 1)
    row = jnp.zeros((1, 128), jnp.int32)
    for s in range(OWN):
        hit = [(at[k] == s).astype(jnp.int32) for k in range(OWN)]
        order[s] = functools.reduce(lambda a, b: a + b, [hit[k] * k for k in range(OWN)])
        name = functools.reduce(lambda a, b: a + b, [hit[k] * d[k] for k in range(OWN)])
        row = jnp.where(lane == s, name, row)
    name_row[...] = row
    pl.semaphore_wait(barrier, GRID - 1 + 2 * (SIDE - 1))

    def remote(src, dst, send, recv, device):
        return pltpu.make_async_remote_copy(
            src_ref=src, dst_ref=dst, send_sem=send, recv_sem=recv, device_id=device, device_id_type=MESH
        )

    def name_y(by, incoming):
        device, other = me.partner(by)
        to = other if incoming else me.p
        return remote(name_row, names.at[me.c, to], send_n.at[0, by], recv_n.at[0, to], device)

    def name_x(by, incoming):
        device, other = me.beside(0, by)
        to = other if incoming else me.x
        return remote(names.at[me.c], names.at[me.z * SIDE + to], send_n.at[1, by], recv_n.at[1, to], device)

    def name_z(by, incoming):
        device, other = me.beside(1, by)
        to = other if incoming else me.z
        mine = names.at[pl.ds(me.z * SIDE, SIDE)]
        return remote(mine, names.at[pl.ds(to * SIDE, SIDE)], send_n.at[2, by], recv_n.at[2, to], device)

    keep_name = pltpu.make_async_copy(name_row, names.at[me.c, me.p], keep_n.at[0])
    keep_name.start()
    for by in range(1, GRID):
        name_y(by, False).start()
    for load in loads:
        load.wait()

    def across(m, by):
        device, other = me.partner(by)
        return remote(act.at[m, other], own.at[m, me.p], send_y.at[m, by], recv_y.at[m, me.p], device)

    def across_in(m, by):
        device, other = me.partner(by)
        return remote(act.at[m, other], own.at[m, other], send_y.at[m, by], recv_y.at[m, other], device)

    def kept(m):
        return pltpu.make_async_copy(act.at[m, me.p], own.at[m, me.p], keep_y.at[m])

    def stay(which, m):
        return pltpu.make_async_copy(own.at[m, :, which], wide[which].at[me.line(which), m], keep_g.at[which, m])

    def gather(which, m, way):
        device, _ = me.beside(which, 1 if way == 0 else SIDE - 1)
        return remote(
            own.at[m, :, which], wide[which].at[me.line(which), m], send_g.at[which, m, way], recv_g.at[which, m, way], device
        )

    def gather_in(which, m, way):
        device, other = me.beside(which, SIDE - 1 if way == 0 else 1)
        return remote(
            own.at[m, :, which], wide[which].at[other, m], send_g.at[which, m, way], recv_g.at[which, m, way], device
        )

    def half(which, line, m, way):
        return wide[which].at[line, m, pl.ds(way * 4, 4)]

    def pass_on(which, m, way):
        _, origin = me.beside(which, SIDE - 1 if way == 0 else 1)
        device, _ = me.beside(which, 1 if way == 0 else SIDE - 1)
        part = half(which, origin, m, way)
        return remote(part, part, send_f.at[which, m, way], recv_f.at[which, m, way], device)

    def pass_on_in(which, m, way):
        device, origin = me.beside(which, 2)
        part = half(which, origin, m, way)
        return remote(part, part, send_f.at[which, m, way], recv_f.at[which, m, way], device)

    both = [(which, way) for which in range(2) for way in range(2)]

    def start_across(m):
        for by in range(1, GRID):
            across(m, by).start()
        kept(m).start()

    def start_gather(m):
        kept(m).wait()
        for by in range(1, GRID):
            across_in(m, by).wait_recv()
        for which, way in both:
            gather(which, m, way).start()
        for which in range(2):
            stay(which, m).start()

    def start_pass(m):
        for which, way in both:
            gather_in(which, m, way).wait_recv()
            pass_on(which, m, way).start()

    def encode(m):
        def after():
            start_across(m)

            @pl.when(m == 0)
            def _():
                keep_name.wait()
                for by in range(1, GRID):
                    name_y(by, True).wait_recv()
                for by in range(1, SIDE):
                    name_x(by, False).start()

            @pl.when(m >= 1)
            def _():
                start_gather(m - 1)

            @pl.when(m == 1)
            def _():
                for by in range(1, SIDE):
                    name_x(by, True).wait_recv()
                for by in range(1, SIDE):
                    name_z(by, False).start()

            @pl.when(m >= 2)
            def _():
                start_pass(m - 2)

        values = [tubes[order[PAIR * m + n]].reshape(1024, 384) for n in range(PAIR)]
        means, scales = encode_pair(
            values, embed_w, embed_g, mixing_w, mixing_g, project_w, spread, act.at[m], after
        )
        for n in range(PAIR):
            mean_s[m, n : n + 1] = means[n]
            scale_s[m, n : n + 1] = scales[n]

    def loop(m, carry):
        encode(m)
        return carry

    lax.fori_loop(0, STEPS, loop, 0)

    def stat_y(by, incoming):
        device, other = me.partner(by)
        to = other if incoming else me.p
        return remote(tile, tiles.at[to], send_s.at[by], recv_s.at[to], device)

    def stat_line(which, by, incoming):
        device, other = me.beside(which, by)
        to = other if incoming else me.line(which)
        return remote(tiles, lines.at[which, to], send_l.at[which, by], recv_l.at[which, to], device)

    mean = mean_s[...].reshape(OWN, C3)
    scale = scale_s[...].reshape(OWN, C3)
    tile[...] = pick_lanes(mean, scale)
    for by in range(1, GRID):
        stat_y(by, False).start()
    keep_tile = pltpu.make_async_copy(tile, tiles.at[me.p], keep_s.at[0])
    keep_tile.start()
    start_gather(STEPS - 1)
    start_pass(STEPS - 2)
    keep_tile.wait()
    for by in range(1, GRID):
        stat_y(by, True).wait_recv()
    for which in range(2):
        for by in range(1, SIDE):
            stat_line(which, by, False).start()
        pltpu.make_async_copy(tiles, lines.at[which, me.line(which)], keep_l.at[which]).start()
    start_pass(STEPS - 1)
    for by in range(1, SIDE):
        name_z(by, True).wait_recv()
    fetch = pltpu.make_async_copy(names, name_s, keep_n.at[1])
    fetch.start()
    fetch.wait()
    for m in range(STEPS):
        for which, way in both:
            pass_on_in(which, m, way).wait_recv()
        for which in range(2):
            stay(which, m).wait()

    def target(which, line):
        return arrived.at[1, :, line] if which else arrived.at[0, line]

    def mark(which, line):
        return marks.at[1, :, line] if which else marks.at[0, line]

    def route(which, by, incoming):
        device, other = me.beside(1 - which, by)
        to = other if incoming else me.line(1 - which)
        return remote(
            packed.at[which, other], target(which, to), send_r.at[which, by], recv_r.at[which, to], device
        )

    def route_mark(which, by, incoming):
        device, other = me.beside(1 - which, by)
        to = other if incoming else me.line(1 - which)
        return remote(
            pack_s.at[which, other], mark(which, to), send_q.at[which, by], recv_q.at[which, to], device
        )

    def stay_route(which):
        line = me.line(1 - which)
        return pltpu.make_async_copy(packed.at[which, line], target(which, line), keep_r.at[which])

    def stay_mark(which):
        line = me.line(1 - which)
        return pltpu.make_async_copy(pack_s.at[which, line], mark(which, line), keep_q.at[which])

    def find(which, other, s, p):
        owner = s * SIDE + me.x if which else me.z * SIDE + s
        wanted = me.z * SIDE + other if which else other * SIDE + me.x
        m, some = jnp.int32(0), jnp.int32(0)
        for k in range(STEPS):
            hit = name_s[owner, p, 0, PAIR * k + which] == wanted
            m, some = jnp.where(hit, k, m), jnp.where(hit, 1, some)
        return m, some

    def pack(which, other):
        def one(s, carry):
            for p in range(GRID):
                m, _ = find(which, other, s, p)
                packed[which, other, s, p] = wide[which][s, m, p]
            return carry

        lax.fori_loop(0, SIDE, one, 0)

    def pack_mark(which, other):
        def one(s, carry):
            for p in range(GRID):
                m, some = find(which, other, s, p)
                line = lines[which, s, p, pl.ds(PAIR * m + which, 1), :]
                pack_s[which, other, s, p : p + 1, :] = jnp.where(lane == 64, some.astype(jnp.float32), line)
            return carry

        lax.fori_loop(0, SIDE, one, 0)

    for by in (2, 1, 3, 0):
        for which in range(2):
            _, other = me.beside(1 - which, by)
            pack(which, other)
            if by:
                route(which, by, False).start()
            else:
                stay_route(which).start()
    for which in range(2):
        pltpu.make_async_copy(tiles, lines.at[which, me.line(which)], keep_l.at[which]).wait()
        for by in range(1, SIDE):
            stat_line(which, by, True).wait_recv()
    for by in (2, 1, 3, 0):
        for which in range(2):
            _, other = me.beside(1 - which, by)
            pack_mark(which, other)
            if by:
                route_mark(which, by, False).start()
            else:
                stay_mark(which).start()

    def count(i, carry):
        c, p = lax.rem(i, SIDE * SIDE), i // (SIDE * SIDE)
        before = jnp.int32(0)
        for k in range(OWN):
            before = before + (name_s[c, p, 0, k] < me.c).astype(jnp.int32)
        parity[i] = before % 2
        return carry

    lax.fori_loop(0, GRID * SIDE * SIDE, count, 0)

    def drain(m, carry):
        for by in range(1, GRID):
            across(m, by).wait_send()
        for which, way in both:
            gather(which, m, way).wait_send()
            pass_on(which, m, way).wait_send()
        return carry

    lax.fori_loop(0, STEPS, drain, 0)
    for by in range(1, GRID):
        name_y(by, False).wait_send()
        stat_y(by, False).wait_send()
    for by in range(1, SIDE):
        name_x(by, False).wait_send()
        name_z(by, False).wait_send()
        for which in range(2):
            stat_line(which, by, False).wait_send()
    for which in range(2):
        stay_route(which).wait()
        stay_mark(which).wait()
        for by in range(1, SIDE):
            route(which, by, True).wait_recv()
            route(which, by, False).wait_send()
            route_mark(which, by, True).wait_recv()
            route_mark(which, by, False).wait_send()


def exchange_call(dest, pixels, embed_w, embed_g, mixing_w, mixing_g, project_w):
    anywhere = pl.BlockSpec(memory_space=pl.ANY)
    inside = pl.BlockSpec(memory_space=pltpu.VMEM)
    scalar = pl.BlockSpec(memory_space=pltpu.SMEM)
    dma = pltpu.SemaphoreType.DMA
    wide = pltpu.VMEM((SIDE, STEPS, GRID, 64, C2), jnp.bfloat16)
    return pl.pallas_call(
        exchange_kernel,
        in_specs=[scalar, anywhere] + [inside] * 5,
        out_specs=[anywhere, anywhere, scalar, anywhere],
        out_shape=[
            jax.ShapeDtypeStruct((2, SIDE, SIDE, GRID, 64, C2), jnp.bfloat16),
            jax.ShapeDtypeStruct((2, SIDE, SIDE, GRID, 128), jnp.float32),
            jax.ShapeDtypeStruct((128,), jnp.int32),
            jax.ShapeDtypeStruct((SIDE * SIDE, GRID, 1, 128), jnp.int32),
        ],
        scratch_shapes=[
            pltpu.VMEM((OWN, 16, 64, 384), jnp.bfloat16),
            pltpu.VMEM((PAIR, GRID, 64, 9 * C1), jnp.bfloat16),
            pltpu.VMEM((STEPS, GRID, PAIR, 64, C2), jnp.bfloat16),
            pltpu.VMEM((STEPS, GRID, PAIR, 64, C2), jnp.bfloat16),
            wide,
            wide,
            pltpu.VMEM((2, SIDE, SIDE, GRID, 64, C2), jnp.bfloat16),
            pltpu.VMEM((STEPS, PAIR, C3), jnp.float32),
            pltpu.VMEM((STEPS, PAIR, C3), jnp.float32),
            pltpu.VMEM((OWN, 128), jnp.float32),
            pltpu.VMEM((GRID, OWN, 128), jnp.float32),
            pltpu.VMEM((2, SIDE, GRID, OWN, 128), jnp.float32),
            pltpu.VMEM((2, SIDE, SIDE, GRID, 128), jnp.float32),
            pltpu.VMEM((1, 128), jnp.int32),
            pltpu.SMEM((SIDE * SIDE, GRID, 1, 128), jnp.int32),
            pltpu.SMEM((OWN,), jnp.int32),
            dma((OWN,)),
            dma((3, GRID)),
            dma((3, GRID)),
            dma((2,)),
            dma((STEPS, GRID)),
            dma((STEPS, GRID)),
            dma((STEPS,)),
            dma((2, STEPS, 2)),
            dma((2, STEPS, 2)),
            dma((2, STEPS)),
            dma((2, STEPS, 2)),
            dma((2, STEPS, 2)),
            dma((GRID,)),
            dma((GRID,)),
            dma((1,)),
            dma((2, SIDE)),
            dma((2, SIDE)),
            dma((2,)),
            dma((2, SIDE)),
            dma((2, SIDE)),
            dma((2,)),
            dma((2, SIDE)),
            dma((2, SIDE)),
            dma((2,)),
        ],
        compiler_params=pltpu.CompilerParams(vmem_limit_bytes=60 * 2**20, collective_id=0, has_side_effects=True),
        name="exchange",
    )(dest, pixels, embed_w, embed_g, mixing_w, mixing_g, project_w)


def spread_groups(st, base):
    lane = lax.broadcasted_iota(jnp.int32, st.shape, 1)
    return jnp.concatenate(
        [jnp.take_along_axis(st, base + 8 * i + lane // 16, axis=1) for i in range(C3 // 128)], axis=1
    )


def decode_kernel(parity, act, marks, weight, gain, out, rows, st):
    step = pl.program_id(0)
    for i in range(8):
        first = parity[step * 8 + i]
        p = step // 2
        for r in range(CAP):
            which = first if r == 0 else 1 - first
            rows[2 * i + r] = act[which, i]
            st[2 * i + r : 2 * i + r + 1, :] = marks[which, i, pl.ds(p, 1), :]
    mean = spread_groups(st[...], 0)
    scale = spread_groups(st[...], 32) * gain[...]
    taken = jnp.broadcast_to(st[:, 64:65], (16, C3)) > 0.5
    for i in range(0, 16, 4):
        values = jnp.dot(rows[i : i + 4].reshape(-1, C2), weight[...], preferred_element_type=jnp.float32)
        for j in range(4):
            n = i + j
            one = (values[64 * j : 64 * j + 64] - mean[n : n + 1]) * scale[n : n + 1]
            out[n] = jnp.where(taken[n : n + 1], one, 0.0).astype(jnp.bfloat16)


def decode_call(parity, act, marks, weight, gain):
    return pl.pallas_call(
        decode_kernel,
        grid_spec=pltpu.PrefetchScalarGridSpec(
            num_scalar_prefetch=1,
            grid=(16,),
            in_specs=[
                pl.BlockSpec((2, 8, None, 64, C2), lambda i, s: (0, i % 2, i // 2, 0, 0)),
                pl.BlockSpec((2, 8, GRID, 128), lambda i, s: (0, i % 2, 0, 0)),
                pl.BlockSpec((C2, C3), lambda i, s: (0, 0)),
                pl.BlockSpec((1, C3), lambda i, s: (0, 0)),
            ],
            out_specs=pl.BlockSpec((16, 64, C3), lambda i, s: (i, 0, 0)),
            scratch_shapes=[pltpu.VMEM((16, 64, C2), jnp.bfloat16), pltpu.VMEM((16, 128), jnp.float32)],
        ),
        out_shape=jax.ShapeDtypeStruct((256, 64, C3), jnp.bfloat16),
        compiler_params=pltpu.CompilerParams(vmem_limit_bytes=60 * 2**20),
        name="decode",
    )(parity, act, marks, weight, gain)


def on_device(
    pixels, destination, embed_weight, embed_gain, mixing_weight, mixing_gain, project_weight, project_gain
):
    arrived, marks, parity, _ = exchange_call(
        destination,
        pixels,
        embed_weight,
        embed_gain.reshape(1, C1),
        mixing_weight.reshape(3, 9 * C1, C2),
        mixing_gain.reshape(1, C2),
        project_weight,
    )
    out = decode_call(
        parity,
        arrived.reshape(2, 16, GRID, 64, C2),
        marks.reshape(2, 16, GRID, 128),
        project_weight,
        project_gain.reshape(1, C3),
    )
    return out.reshape(256, 8, GRID, C3)


def solution(mesh):
    return jax.shard_map(
        on_device,
        mesh=mesh,
        in_specs=(P(("clip", "patch"), None, None, None), P(("clip", "patch"), None), P(), P(), P(), P(), P(), P()),
        out_specs=P("clip", None, "patch", None),
        check_vma=False,
    )
```

time: 153 us -> 133 us (0.87)
  Pallas kernels: 143 us -> 131 us
  other arithmetic: 6.44 us -> 0 us
    pallas_call x2 -> x1, Pallas kernels: 125 us -> 113 us  [exchange_call(): pl.pallas_call(exchange_kernel, in_specs=[scalar, anywhere] + [inside] *...]
    reduce_sum x6 -> x0, other arithmetic: 3.08 us -> none  [the longest x1 1.36 us: on_device(): in_order = jnp.sum(jnp.where(hits, targets[None, :], 0), axis=1)]
    convert_element_type x4 -> x0, local copies, waits for them, and re-layouts: 1.57 us -> none  [the longest x2 1.31 us: on_device(): named = jnp.round(stats[:, :, :, 64]).astype(jnp.int32)]
where the time goes in v2:
time: 133 us; the launch traced here: 132 us
  Pallas kernels  131 us (98%)
    pallas_call x1, Pallas kernels, exchange_call(): pl.pallas_call(exchange_kernel, in_specs=[scalar, anywhere] + [inside] *...  113 us
    pallas_call x1, Pallas kernels, decode_call(): pl.pallas_call(decode_kernel, grid_spec=pltpu.PrefetchScalarGridSpec(num_...  17.3 us

profile of v2, /device:TPU:1, one launch (start us, length us, event | category | flops | bytes accessed | tf_op | source)
XLA Modules:
  0.0 132.0 jit_solution(9902985256770533838)
XLA Ops:
  0.0 1.3 %copy.9.dest = s32[8,1]{1,0:T(8,128)} copy(s32[8,1]{0,1:T(1,128)} %param.9) | data formatting | bytes 64 | tf_op args[1]
  1.3 113.4 %exchange.1 = (bf16[2,4,4,8,64,256]{5,4,3,2,1,0:T(8,128)(2,1)}, f32[2,4,4,8,128]{4,3,2,1,0:T(8,128)}, s32[128]{0:T(128)}, s32[16,8,1,128]{3,2,1,0:T(1,128)}) custom-call(s32[8,1]{1,0:T(8,128)} %copy.9.dest, bf16[8,16,64,384]{3,2,1,0:T(8,128)(2,1)} %pixels.1, bf16[384,128]{1,0:T(8,128)(2,1)} %embed_w.1, f32[1,128]{1,0:T(1,128)} %bitcast.12, ...), custom_call_target="tpu_custom_call" | custom-call | tf_op jit(solution)/shard_map/exchange/pallas_call | solution.py:457
  114.7 17.3 %decode.1 = bf16[256,64,512]{2,1,0:T(8,128)(2,1)} custom-call(s32[128]{0:T(128)} %get-tuple-element.8.parity, bf16[2,16,8,64,256]{4,3,2,1,0:T(8,128)(2,1)} %bitcast.7, f32[2,16,8,128]{3,2,1,0:T(8,128)} %bitcast.9, bf16[256,512]{1,0:T(8,128)(2,1)} %weight.1, f32[1,512]{1,0:T(1,128)} %bitcast.10), custom_call_target="tpu_custom_call" | custom-call | tf_op jit(solution)/shard_map/decode/pallas_call | solution.py:542

commit v3 on v2

--- a/solution.py
+++ b/solution.py
@@ -134,7 +134,7 @@
 
 def exchange_kernel(
     dest, pixels, embed_w, embed_g, mixing_w, mixing_g, project_w,
-    arrived, marks, parity, names,
+    arrived, marks, state, names,
     tubes, spread, act, own, wide_x, wide_z, packed, mean_s, scale_s, tile, tiles, lines, pack_s, name_row, name_s, order,
     pix_sem, send_n, recv_n, keep_n, send_y, recv_y, keep_y, send_g, recv_g, keep_g, send_f, recv_f, send_s, recv_s, keep_s,
     send_l, recv_l, keep_l, send_r, recv_r, keep_r, send_q, recv_q, keep_q,
@@ -151,7 +151,7 @@
         for by in range(1, SIDE):
             pl.semaphore_signal(barrier, inc=1, device_id=me.beside(which, by)[0], device_id_type=MESH)
 
-    d = [dest[k, 0] for k in range(OWN)]
+    d = [dest[0, k] for k in range(OWN)]
     at = []
     for k in range(OWN):
         ahead = [((d[j] <= d[k]) if j < k else (d[j] < d[k])).astype(jnp.int32) for j in range(OWN) if j != k]
@@ -365,16 +365,15 @@
     def find(which, other, s, p):
         owner = s * SIDE + me.x if which else me.z * SIDE + s
         wanted = me.z * SIDE + other if which else other * SIDE + me.x
-        m, some = jnp.int32(0), jnp.int32(0)
+        m = jnp.int32(0)
         for k in range(STEPS):
-            hit = name_s[owner, p, 0, PAIR * k + which] == wanted
-            m, some = jnp.where(hit, k, m), jnp.where(hit, 1, some)
-        return m, some
+            m = jnp.where(name_s[owner, p, 0, PAIR * k + which] == wanted, k, m)
+        return m
 
     def pack(which, other):
         def one(s, carry):
             for p in range(GRID):
-                m, _ = find(which, other, s, p)
+                m = find(which, other, s, p)
                 packed[which, other, s, p] = wide[which][s, m, p]
             return carry
 
@@ -383,9 +382,8 @@
     def pack_mark(which, other):
         def one(s, carry):
             for p in range(GRID):
-                m, some = find(which, other, s, p)
-                line = lines[which, s, p, pl.ds(PAIR * m + which, 1), :]
-                pack_s[which, other, s, p : p + 1, :] = jnp.where(lane == 64, some.astype(jnp.float32), line)
+                m = find(which, other, s, p)
+                pack_s[which, other, s, p : p + 1, :] = lines[which, s, p, pl.ds(PAIR * m + which, 1), :]
             return carry
 
         lax.fori_loop(0, SIDE, one, 0)
@@ -413,10 +411,12 @@
 
     def count(i, carry):
         c, p = lax.rem(i, SIDE * SIDE), i // (SIDE * SIDE)
-        before = jnp.int32(0)
+        before, number = jnp.int32(0), jnp.int32(0)
         for k in range(OWN):
-            before = before + (name_s[c, p, 0, k] < me.c).astype(jnp.int32)
-        parity[i] = before % 2
+            name = name_s[c, p, 0, k]
+            before = before + (name < me.c).astype(jnp.int32)
+            number = number + (name == me.c).astype(jnp.int32)
+        state[i] = before % 2 + 2 * number
         return carry
 
     lax.fori_loop(0, GRID * SIDE * SIDE, count, 0)
@@ -518,52 +518,80 @@
     )
 
 
-def decode_kernel(parity, act, marks, weight, gain, out, rows, st):
-    step = pl.program_id(0)
-    for i in range(8):
-        first = parity[step * 8 + i]
-        p = step // 2
-        for r in range(CAP):
-            which = first if r == 0 else 1 - first
-            rows[2 * i + r] = act[which, i]
-            st[2 * i + r : 2 * i + r + 1, :] = marks[which, i, pl.ds(p, 1), :]
-    mean = spread_groups(st[...], 0)
-    scale = spread_groups(st[...], 32) * gain[...]
-    taken = jnp.broadcast_to(st[:, 64:65], (16, C3)) > 0.5
-    for i in range(0, 16, 4):
-        values = jnp.dot(rows[i : i + 4].reshape(-1, C2), weight[...], preferred_element_type=jnp.float32)
-        for j in range(4):
-            n = i + j
-            one = (values[64 * j : 64 * j + 64] - mean[n : n + 1]) * scale[n : n + 1]
-            out[n] = jnp.where(taken[n : n + 1], one, 0.0).astype(jnp.bfloat16)
-
-
-def decode_call(parity, act, marks, weight, gain):
+PART = 16
+PARTS = 256 // PART
+
+
+def decode_kernel(state, arrived, marks, weight, gain, out, act, ready, rows, st, in_sem, out_sem):
+    def fetch(i):
+        p, c = i // 2, pl.ds(lax.rem(i, 2) * 8, 8)
+        return pltpu.make_async_copy(arrived.at[:, c, p], act.at[i], in_sem.at[i])
+
+    def put(i):
+        return pltpu.make_async_copy(ready.at[i], out.at[pl.ds(i * PART, PART)], out_sem.at[i])
+
+    def begin(i, carry):
+        fetch(i).start()
+        return carry
+
+    lax.fori_loop(0, PARTS, begin, 0)
+
+    def work(i, carry):
+        p, c = i // 2, lax.rem(i, 2) * 8
+        fetch(i).wait()
+        for j in range(8):
+            first, number = state[i * 8 + j] % 2, state[i * 8 + j] // 2
+            for r in range(CAP):
+                which = first if r == 0 else 1 - first
+                n = CAP * j + r
+                rows[n] = jnp.where(number > r, act[i, which, j], jnp.zeros((64, C2), jnp.bfloat16))
+                st[n : n + 1, :] = jnp.where(number > r, marks[which, c + j, pl.ds(p, 1), :], 0.0)
+        mean = spread_groups(st[...], 0)
+        scale = spread_groups(st[...], 32) * gain[...]
+        for k in range(0, PART, 4):
+            values = jnp.dot(rows[k : k + 4].reshape(-1, C2), weight[...], preferred_element_type=jnp.float32)
+            for j in range(4):
+                n = k + j
+                one = (values[64 * j : 64 * j + 64] - mean[n : n + 1]) * scale[n : n + 1]
+                ready[i, n] = one.astype(jnp.bfloat16)
+        put(i).start()
+        return carry
+
+    lax.fori_loop(0, PARTS, work, 0)
+
+    def finish(i, carry):
+        put(i).wait()
+        return carry
+
+    lax.fori_loop(0, PARTS, finish, 0)
+
+
+def decode_call(state, arrived, marks, weight, gain):
+    anywhere = pl.BlockSpec(memory_space=pl.ANY)
+    inside = pl.BlockSpec(memory_space=pltpu.VMEM)
     return pl.pallas_call(
         decode_kernel,
-        grid_spec=pltpu.PrefetchScalarGridSpec(
-            num_scalar_prefetch=1,
-            grid=(16,),
-            in_specs=[
-                pl.BlockSpec((2, 8, None, 64, C2), lambda i, s: (0, i % 2, i // 2, 0, 0)),
-                pl.BlockSpec((2, 8, GRID, 128), lambda i, s: (0, i % 2, 0, 0)),
-                pl.BlockSpec((C2, C3), lambda i, s: (0, 0)),
-                pl.BlockSpec((1, C3), lambda i, s: (0, 0)),
-            ],
-            out_specs=pl.BlockSpec((16, 64, C3), lambda i, s: (i, 0, 0)),
-            scratch_shapes=[pltpu.VMEM((16, 64, C2), jnp.bfloat16), pltpu.VMEM((16, 128), jnp.float32)],
-        ),
+        in_specs=[pl.BlockSpec(memory_space=pltpu.SMEM), anywhere, inside, inside, inside],
+        out_specs=anywhere,
+        scratch_shapes=[
+            pltpu.VMEM((PARTS, 2, 8, 64, C2), jnp.bfloat16),
+            pltpu.VMEM((PARTS, PART, 64, C3), jnp.bfloat16),
+            pltpu.VMEM((PART, 64, C2), jnp.bfloat16),
+            pltpu.VMEM((PART, 128), jnp.float32),
+            pltpu.SemaphoreType.DMA((PARTS,)),
+            pltpu.SemaphoreType.DMA((PARTS,)),
+        ],
         out_shape=jax.ShapeDtypeStruct((256, 64, C3), jnp.bfloat16),
         compiler_params=pltpu.CompilerParams(vmem_limit_bytes=60 * 2**20),
         name="decode",
-    )(parity, act, marks, weight, gain)
+    )(state, arrived, marks, weight, gain)
 
 
 def on_device(
     pixels, destination, embed_weight, embed_gain, mixing_weight, mixing_gain, project_weight, project_gain
 ):
-    arrived, marks, parity, _ = exchange_call(
-        destination,
+    arrived, marks, state, _ = exchange_call(
+        destination.reshape(1, OWN),
         pixels,
         embed_weight,
         embed_gain.reshape(1, C1),
@@ -572,7 +600,7 @@
         project_weight,
     )
     out = decode_call(
-        parity,
+        state,
         arrived.reshape(2, 16, GRID, 64, C2),
         marks.reshape(2, 16, GRID, 128),
         project_weight,

time: 133 us -> 125 us (0.940)
  Pallas kernels: 131 us -> 125 us
    pallas_call x1, Pallas kernels: 17.3 us -> 11.3 us  [decode_call(): pl.pallas_call(decode_kernel, in_specs=[pl.BlockSpec(memory_space=pltpu.S...]
where the time goes in v3:
time: 125 us
  Pallas kernels  125 us (100%)
    pallas_call x1, Pallas kernels, exchange_call(): pl.pallas_call(exchange_kernel, in_specs=[scalar, anywhere] + [inside] *...  113 us
    pallas_call x1, Pallas kernels, decode_call(): pl.pallas_call(decode_kernel, in_specs=[pl.BlockSpec(memory_space=pltpu.S...  11.3 us

profile of v3, /device:TPU:1, one launch (start us, length us, event | category | flops | bytes accessed | tf_op | source)
XLA Modules:
  0.0 124.6 jit_solution(7909710173468600098)
XLA Ops:
  0.0 113.4 %exchange.1 = (bf16[2,4,4,8,64,256]{5,4,3,2,1,0:T(8,128)(2,1)}, f32[2,4,4,8,128]{4,3,2,1,0:T(8,128)}, s32[128]{0:T(128)}, s32[16,8,1,128]{3,2,1,0:T(1,128)}) custom-call(s32[1,8]{1,0:T(1,128)} %bitcast.13, bf16[8,16,64,384]{3,2,1,0:T(8,128)(2,1)} %pixels.1, bf16[384,128]{1,0:T(8,128)(2,1)} %embed_w.1, f32[1,128]{1,0:T(1,128)} %bitcast.14, ...), custom_call_target="tpu_custom_call" | custom-call | tf_op jit(solution)/shard_map/exchange/pallas_call | solution.py:457
  113.4 11.3 %decode.1 = bf16[256,64,512]{2,1,0:T(8,128)(2,1)} custom-call(s32[128]{0:T(128)} %get-tuple-element.8.state, bf16[2,16,8,64,256]{4,3,2,1,0:T(8,128)(2,1)} %bitcast.8, f32[2,16,8,128]{3,2,1,0:T(8,128)} %bitcast.10, bf16[256,512]{1,0:T(8,128)(2,1)} %weight.1, f32[1,512]{1,0:T(1,128)} %bitcast.11), custom_call_target="tpu_custom_call" | custom-call | tf_op jit(solution)/shard_map/decode/pallas_call | solution.py:572

commit v4 on v3

--- a/solution.py
+++ b/solution.py
@@ -135,12 +135,12 @@
 def exchange_kernel(
     dest, pixels, embed_w, embed_g, mixing_w, mixing_g, project_w,
     arrived, marks, state, names,
-    tubes, spread, act, own, wide_x, wide_z, packed, mean_s, scale_s, tile, tiles, lines, pack_s, name_row, name_s, order,
-    pix_sem, send_n, recv_n, keep_n, send_y, recv_y, keep_y, send_g, recv_g, keep_g, send_f, recv_f, send_s, recv_s, keep_s,
+    tubes, spread, act, own, near_x, near_z, far_x, far_z, packed, mean_s, scale_s, tile, tiles, lines, pack_s, name_row, name_s, order,
+    pix_sem, send_n, recv_n, keep_n, send_y, recv_y, keep_y, send_g, recv_g, send_f, recv_f, send_s, recv_s, keep_s,
     send_l, recv_l, keep_l, send_r, recv_r, keep_r, send_q, recv_q, keep_q,
 ):
     me = Place()
-    wide = (wide_x, wide_z)
+    near, far = (near_x, near_z), (far_x, far_z)
     loads = [pltpu.make_async_copy(pixels.at[n], tubes.at[n], pix_sem.at[n]) for n in range(OWN)]
     for load in loads:
         load.start()
@@ -205,34 +205,18 @@
     def kept(m):
         return pltpu.make_async_copy(act.at[m, me.p], own.at[m, me.p], keep_y.at[m])
 
-    def stay(which, m):
-        return pltpu.make_async_copy(own.at[m, :, which], wide[which].at[me.line(which), m], keep_g.at[which, m])
-
     def gather(which, m, way):
         device, _ = me.beside(which, 1 if way == 0 else SIDE - 1)
         return remote(
-            own.at[m, :, which], wide[which].at[me.line(which), m], send_g.at[which, m, way], recv_g.at[which, m, way], device
+            own.at[m, :, which], near[which].at[way, m], send_g.at[which, m, way], recv_g.at[which, m, way], device
         )
 
-    def gather_in(which, m, way):
-        device, other = me.beside(which, SIDE - 1 if way == 0 else 1)
+    def pass_on(which, m, way):
+        device, _ = me.beside(which, 1 if way == 0 else SIDE - 1)
+        part = pl.ds(way * 4, 4)
         return remote(
-            own.at[m, :, which], wide[which].at[other, m], send_g.at[which, m, way], recv_g.at[which, m, way], device
+            near[which].at[way, m, part], far[which].at[m, part], send_f.at[which, m, way], recv_f.at[which, m, way], device
         )
-
-    def half(which, line, m, way):
-        return wide[which].at[line, m, pl.ds(way * 4, 4)]
-
-    def pass_on(which, m, way):
-        _, origin = me.beside(which, SIDE - 1 if way == 0 else 1)
-        device, _ = me.beside(which, 1 if way == 0 else SIDE - 1)
-        part = half(which, origin, m, way)
-        return remote(part, part, send_f.at[which, m, way], recv_f.at[which, m, way], device)
-
-    def pass_on_in(which, m, way):
-        device, origin = me.beside(which, 2)
-        part = half(which, origin, m, way)
-        return remote(part, part, send_f.at[which, m, way], recv_f.at[which, m, way], device)
 
     both = [(which, way) for which in range(2) for way in range(2)]
 
@@ -247,12 +231,10 @@
             across_in(m, by).wait_recv()
         for which, way in both:
             gather(which, m, way).start()
-        for which in range(2):
-            stay(which, m).start()
 
     def start_pass(m):
         for which, way in both:
-            gather_in(which, m, way).wait_recv()
+            gather(which, m, way).wait_recv()
             pass_on(which, m, way).start()
 
     def encode(m):
@@ -314,6 +296,10 @@
     keep_tile = pltpu.make_async_copy(tile, tiles.at[me.p], keep_s.at[0])
     keep_tile.start()
     start_gather(STEPS - 1)
+    for by in range(1, SIDE):
+        name_z(by, True).wait_recv()
+    fetch_names = pltpu.make_async_copy(names, name_s, keep_n.at[1])
+    fetch_names.start()
     start_pass(STEPS - 2)
     keep_tile.wait()
     for by in range(1, GRID):
@@ -322,29 +308,20 @@
         for by in range(1, SIDE):
             stat_line(which, by, False).start()
         pltpu.make_async_copy(tiles, lines.at[which, me.line(which)], keep_l.at[which]).start()
-    start_pass(STEPS - 1)
-    for by in range(1, SIDE):
-        name_z(by, True).wait_recv()
-    fetch = pltpu.make_async_copy(names, name_s, keep_n.at[1])
-    fetch.start()
-    fetch.wait()
-    for m in range(STEPS):
-        for which, way in both:
-            pass_on_in(which, m, way).wait_recv()
-        for which in range(2):
-            stay(which, m).wait()
-
-    def target(which, line):
-        return arrived.at[1, :, line] if which else arrived.at[0, line]
+    def target(which, line, s):
+        return arrived.at[1, s, line] if which else arrived.at[0, line, s]
 
     def mark(which, line):
         return marks.at[1, :, line] if which else marks.at[0, line]
 
-    def route(which, by, incoming):
+    def source(which, kind):
+        return lax.rem(me.line(which) + (0, SIDE - 1, 1, 2)[kind], SIDE)
+
+    def route(which, by, kind, incoming):
         device, other = me.beside(1 - which, by)
-        to = other if incoming else me.line(1 - which)
+        to, s = other if incoming else me.line(1 - which), source(which, kind)
         return remote(
-            packed.at[which, other], target(which, to), send_r.at[which, by], recv_r.at[which, to], device
+            packed.at[which, other, s], target(which, to, s), send_r.at[which, by, kind], recv_r.at[which, to, kind], device
         )
 
     def route_mark(which, by, incoming):
@@ -354,9 +331,9 @@
             pack_s.at[which, other], mark(which, to), send_q.at[which, by], recv_q.at[which, to], device
         )
 
-    def stay_route(which):
-        line = me.line(1 - which)
-        return pltpu.make_async_copy(packed.at[which, line], target(which, line), keep_r.at[which])
+    def stay_route(which, kind):
+        line, s = me.line(1 - which), source(which, kind)
+        return pltpu.make_async_copy(packed.at[which, line, s], target(which, line, s), keep_r.at[which, kind])
 
     def stay_mark(which):
         line = me.line(1 - which)
@@ -370,14 +347,31 @@
             m = jnp.where(name_s[owner, p, 0, PAIR * k + which] == wanted, k, m)
         return m
 
-    def pack(which, other):
-        def one(s, carry):
-            for p in range(GRID):
-                m = find(which, other, s, p)
-                packed[which, other, s, p] = wide[which][s, m, p]
+    def pack(which, other, kind):
+        s = source(which, kind)
+
+        def one(p, carry):
+            m = find(which, other, s, p)
+            if kind == 0:
+                packed[which, other, s, p] = own[m, p, which]
+            elif kind == 3:
+                packed[which, other, s, p] = far[which][m, p]
+            else:
+                packed[which, other, s, p] = near[which][kind - 1, m, p]
             return carry
 
-        lax.fori_loop(0, SIDE, one, 0)
+        lax.fori_loop(0, GRID, one, 0)
+
+    def start_route(kinds, hops):
+        for by in hops:
+            for which in range(2):
+                for kind in kinds:
+                    _, other = me.beside(1 - which, by)
+                    pack(which, other, kind)
+                    if by:
+                        route(which, by, kind, False).start()
+                    else:
+                        stay_route(which, kind).start()
 
     def pack_mark(which, other):
         def one(s, carry):
@@ -388,14 +382,15 @@
 
         lax.fori_loop(0, SIDE, one, 0)
 
-    for by in (2, 1, 3, 0):
-        for which in range(2):
-            _, other = me.beside(1 - which, by)
-            pack(which, other)
-            if by:
-                route(which, by, False).start()
-            else:
-                stay_route(which).start()
+    fetch_names.wait()
+    start_route((0,), (2, 1, 3))
+    start_pass(STEPS - 1)
+    start_route((1, 2), (2, 1, 3))
+    for m in range(STEPS):
+        for which, way in both:
+            pass_on(which, m, way).wait_recv()
+    start_route((3,), (2, 1, 3))
+    start_route((0, 1, 2, 3), (0,))
     for which in range(2):
         pltpu.make_async_copy(tiles, lines.at[which, me.line(which)], keep_l.at[which]).wait()
         for by in range(1, SIDE):
@@ -439,11 +434,13 @@
         for which in range(2):
             stat_line(which, by, False).wait_send()
     for which in range(2):
-        stay_route(which).wait()
         stay_mark(which).wait()
+        for kind in range(SIDE):
+            stay_route(which, kind).wait()
+            for by in range(1, SIDE):
+                route(which, by, kind, True).wait_recv()
+                route(which, by, kind, False).wait_send()
         for by in range(1, SIDE):
-            route(which, by, True).wait_recv()
-            route(which, by, False).wait_send()
             route_mark(which, by, True).wait_recv()
             route_mark(which, by, False).wait_send()
 
@@ -453,7 +450,8 @@
     inside = pl.BlockSpec(memory_space=pltpu.VMEM)
     scalar = pl.BlockSpec(memory_space=pltpu.SMEM)
     dma = pltpu.SemaphoreType.DMA
-    wide = pltpu.VMEM((SIDE, STEPS, GRID, 64, C2), jnp.bfloat16)
+    near = pltpu.VMEM((2, STEPS, GRID, 64, C2), jnp.bfloat16)
+    far = pltpu.VMEM((STEPS, GRID, 64, C2), jnp.bfloat16)
     return pl.pallas_call(
         exchange_kernel,
         in_specs=[scalar, anywhere] + [inside] * 5,
@@ -469,8 +467,10 @@
             pltpu.VMEM((PAIR, GRID, 64, 9 * C1), jnp.bfloat16),
             pltpu.VMEM((STEPS, GRID, PAIR, 64, C2), jnp.bfloat16),
             pltpu.VMEM((STEPS, GRID, PAIR, 64, C2), jnp.bfloat16),
-            wide,
-            wide,
+            near,
+            near,
+            far,
+            far,
             pltpu.VMEM((2, SIDE, SIDE, GRID, 64, C2), jnp.bfloat16),
             pltpu.VMEM((STEPS, PAIR, C3), jnp.float32),
             pltpu.VMEM((STEPS, PAIR, C3), jnp.float32),
@@ -490,7 +490,6 @@
             dma((STEPS,)),
             dma((2, STEPS, 2)),
             dma((2, STEPS, 2)),
-            dma((2, STEPS)),
             dma((2, STEPS, 2)),
             dma((2, STEPS, 2)),
             dma((GRID,)),
@@ -499,9 +498,9 @@
             dma((2, SIDE)),
             dma((2, SIDE)),
             dma((2,)),
+            dma((2, SIDE, SIDE)),
+            dma((2, SIDE, SIDE)),
             dma((2, SIDE)),
-            dma((2, SIDE)),
-            dma((2,)),
             dma((2, SIDE)),
             dma((2, SIDE)),
             dma((2,)),
@@ -518,14 +517,13 @@
     )
 
 
-PART = 16
+PART = 32
 PARTS = 256 // PART
 
 
 def decode_kernel(state, arrived, marks, weight, gain, out, act, ready, rows, st, in_sem, out_sem):
     def fetch(i):
-        p, c = i // 2, pl.ds(lax.rem(i, 2) * 8, 8)
-        return pltpu.make_async_copy(arrived.at[:, c, p], act.at[i], in_sem.at[i])
+        return pltpu.make_async_copy(arrived.at[:, :, i], act.at[i], in_sem.at[i])
 
     def put(i):
         return pltpu.make_async_copy(ready.at[i], out.at[pl.ds(i * PART, PART)], out_sem.at[i])
@@ -537,15 +535,14 @@
     lax.fori_loop(0, PARTS, begin, 0)
 
     def work(i, carry):
-        p, c = i // 2, lax.rem(i, 2) * 8
         fetch(i).wait()
-        for j in range(8):
-            first, number = state[i * 8 + j] % 2, state[i * 8 + j] // 2
+        for j in range(16):
+            first, number = state[i * 16 + j] % 2, state[i * 16 + j] // 2
             for r in range(CAP):
                 which = first if r == 0 else 1 - first
                 n = CAP * j + r
                 rows[n] = jnp.where(number > r, act[i, which, j], jnp.zeros((64, C2), jnp.bfloat16))
-                st[n : n + 1, :] = jnp.where(number > r, marks[which, c + j, pl.ds(p, 1), :], 0.0)
+                st[n : n + 1, :] = jnp.where(number > r, marks[which, j, pl.ds(i, 1), :], 0.0)
         mean = spread_groups(st[...], 0)
         scale = spread_groups(st[...], 32) * gain[...]
         for k in range(0, PART, 4):
@@ -574,7 +571,7 @@
         in_specs=[pl.BlockSpec(memory_space=pltpu.SMEM), anywhere, inside, inside, inside],
         out_specs=anywhere,
         scratch_shapes=[
-            pltpu.VMEM((PARTS, 2, 8, 64, C2), jnp.bfloat16),
+            pltpu.VMEM((PARTS, 2, 16, 64, C2), jnp.bfloat16),
             pltpu.VMEM((PARTS, PART, 64, C3), jnp.bfloat16),
             pltpu.VMEM((PART, 64, C2), jnp.bfloat16),
             pltpu.VMEM((PART, 128), jnp.float32),

time: 125 us -> 120 us (0.960)
  Pallas kernels: 125 us -> 120 us
    pallas_call x1, Pallas kernels: 113 us -> 110 us  [exchange_call(): pl.pallas_call(exchange_kernel, in_specs=[scalar, anywhere] + [inside] *...]
where the time goes in v4:
time: 120 us
  Pallas kernels  120 us (100%)
    pallas_call x1, Pallas kernels, exchange_call(): pl.pallas_call(exchange_kernel, in_specs=[scalar, anywhere] + [inside] *...  110 us
    pallas_call x1, Pallas kernels, decode_call(): pl.pallas_call(decode_kernel, in_specs=[pl.BlockSpec(memory_space=pltpu.S...  10.5 us

profile of v4, /device:TPU:1, one launch (start us, length us, event | category | flops | bytes accessed | tf_op | source)
XLA Modules:
  0.0 120.1 jit_solution(9088730616251184806)
XLA Ops:
  0.0 109.6 %exchange.1 = (bf16[2,4,4,8,64,256]{5,4,3,2,1,0:T(8,128)(2,1)}, f32[2,4,4,8,128]{4,3,2,1,0:T(8,128)}, s32[128]{0:T(128)}, s32[16,8,1,128]{3,2,1,0:T(1,128)}) custom-call(s32[1,8]{1,0:T(1,128)} %bitcast.13, bf16[8,16,64,384]{3,2,1,0:T(8,128)(2,1)} %pixels.1, bf16[384,128]{1,0:T(8,128)(2,1)} %embed_w.1, f32[1,128]{1,0:T(1,128)} %bitcast.14, ...), custom_call_target="tpu_custom_call" | custom-call | tf_op jit(solution)/shard_map/exchange/pallas_call | solution.py:455
  109.6 10.5 %decode.1 = bf16[256,64,512]{2,1,0:T(8,128)(2,1)} custom-call(s32[128]{0:T(128)} %get-tuple-element.8.state, bf16[2,16,8,64,256]{4,3,2,1,0:T(8,128)(2,1)} %bitcast.8, f32[2,16,8,128]{3,2,1,0:T(8,128)} %bitcast.10, bf16[256,512]{1,0:T(8,128)(2,1)} %weight.1, f32[1,512]{1,0:T(1,128)} %bitcast.11), custom_call_target="tpu_custom_call" | custom-call | tf_op jit(solution)/shard_map/decode/pallas_call | solution.py:569

commit v5 on v4

--- a/solution.py
+++ b/solution.py
@@ -63,46 +63,41 @@
     return h + h * jnp.tanh(h)
 
 
-def encode_pair(tubes, embed_w, embed_g, mixing_w, mixing_g, project_w, spread, act, after):
-    first = [jnp.dot(t, embed_w[...], preferred_element_type=jnp.float32) for t in tubes]
-    means, scales = moments(first)
+def encode_pair(tubes, embed_w, embed_g, mixing_w, mixing_g, project_w, first, spread, second, act, after):
     for n in range(PAIR):
-        wide = silu((first[n] - means[n]) * (scales[n] * embed_g[...]))
-        wide = wide.reshape(8, 2, GRID, GRID, C1)
-        even, odd = wide[:, 0], wide[:, 1]
-        place = lax.broadcasted_iota(jnp.int32, (8 * GRID * GRID, C1), 0) % GRID
-        for j in range(3):
-            for a, source in ((1, even), (2, odd)):
-                flat = source.reshape(8 * GRID * GRID, C1)
-                moved = source
-                if j == 0:
-                    moved = jnp.where(place == 0, 0.0, pltpu.roll(flat, 1, 0))
-                elif j == 2:
-                    moved = jnp.where(place == GRID - 1, 0.0, pltpu.roll(flat, 8 * GRID * GRID - 1, 0))
-                moved = moved.reshape(8, GRID, GRID, C1)
-                low = (j * 3 + a) * C1
-                for y in range(GRID):
-                    block = moved[:, y].reshape(64, C1)
-                    spread[n, y, :, low : low + C1] = block.astype(jnp.bfloat16)
-                    if a == 2:
-                        prior = jnp.concatenate([jnp.zeros((GRID, C1), jnp.float32), block[:-GRID]], axis=0)
-                        spread[n, y, :, low - 2 * C1 : low - C1] = prior.astype(jnp.bfloat16)
-    second = []
+        wide = jnp.dot(tubes[n], embed_w[...], preferred_element_type=jnp.float32)
+        first[n] = wide.reshape(16, GRID, GRID, C1)
+    means, scales = moments([first[n].reshape(1024, C1) for n in range(PAIR)])
+    place = lax.broadcasted_iota(jnp.int32, (8, GRID, C1), 1)
     for n in range(PAIR):
-        mid = jnp.dot(spread[n].reshape(512, 9 * C1), mixing_w[1], preferred_element_type=jnp.float32)
-        low = jnp.dot(spread[n, 0:7].reshape(448, 9 * C1), mixing_w[0], preferred_element_type=jnp.float32)
-        high = jnp.dot(spread[n, 1:8].reshape(448, 9 * C1), mixing_w[2], preferred_element_type=jnp.float32)
-        none = jnp.zeros((64, C2), jnp.float32)
-        second.append(
-            mid + jnp.concatenate([none, low], axis=0) + jnp.concatenate([high, none], axis=0)
-        )
-    means, scales = moments(second)
-    acts = []
+        gain = scales[n] * embed_g[...]
+        for y in range(GRID):
+            part = silu((first[n, :, y] - means[n]) * gain).reshape(8, 2, GRID, C1)
+            for j in range(3):
+                low = j * 3 * C1
+                moved = []
+                for a in range(2):
+                    one = part[:, a]
+                    if j == 0:
+                        one = jnp.where(place == 0, 0.0, pltpu.roll(one, 1, 1))
+                    elif j == 2:
+                        one = jnp.where(place == GRID - 1, 0.0, pltpu.roll(one, GRID - 1, 1))
+                    moved.append(one)
+                prior = jnp.concatenate([jnp.zeros((1, GRID, C1), jnp.float32), moved[1][:-1]], axis=0)
+                for a, one in enumerate((prior, moved[0], moved[1])):
+                    spread[n, y, :, low + a * C1 : low + (a + 1) * C1] = one.reshape(64, C1).astype(jnp.bfloat16)
+        second[n] = jnp.dot(spread[n].reshape(512, 9 * C1), mixing_w[1], preferred_element_type=jnp.float32)
+        second[n, 64:512] += jnp.dot(spread[n, 0:7].reshape(448, 9 * C1), mixing_w[0], preferred_element_type=jnp.float32)
+        second[n, 0:448] += jnp.dot(spread[n, 1:8].reshape(448, 9 * C1), mixing_w[2], preferred_element_type=jnp.float32)
     for n in range(PAIR):
-        acts.append(silu((second[n] - means[n]) * (scales[n] * mixing_g[...])).astype(jnp.bfloat16))
-        act[:, n] = acts[n].reshape(GRID, 64, C2)
+        (mean,), (scale,) = moments([second[n]])
+        gain = scale * mixing_g[...]
+        for y in range(GRID):
+            act[y, n] = silu((second[n, 64 * y : 64 * y + 64] - mean) * gain).astype(jnp.bfloat16)
     after()
-    return moments([jnp.dot(a, project_w[...], preferred_element_type=jnp.float32) for a in acts])
+    return moments(
+        [jnp.dot(act[:, n].reshape(512, C2), project_w[...], preferred_element_type=jnp.float32) for n in range(PAIR)]
+    )
 
 
 def pick_lanes(mean, scale):
@@ -135,7 +130,7 @@
 def exchange_kernel(
     dest, pixels, embed_w, embed_g, mixing_w, mixing_g, project_w,
     arrived, marks, state, names,
-    tubes, spread, act, own, near_x, near_z, far_x, far_z, packed, mean_s, scale_s, tile, tiles, lines, pack_s, name_row, name_s, order,
+    tubes, first, spread, second, act, own, near_x, near_z, far_x, far_z, packed, mean_s, scale_s, tile, tiles, lines, pack_s, name_row, name_s, order,
     pix_sem, send_n, recv_n, keep_n, send_y, recv_y, keep_y, send_g, recv_g, send_f, recv_f, send_s, recv_s, keep_s,
     send_l, recv_l, keep_l, send_r, recv_r, keep_r, send_q, recv_q, keep_q,
 ):
@@ -266,7 +261,7 @@
 
         values = [tubes[order[PAIR * m + n]].reshape(1024, 384) for n in range(PAIR)]
         means, scales = encode_pair(
-            values, embed_w, embed_g, mixing_w, mixing_g, project_w, spread, act.at[m], after
+            values, embed_w, embed_g, mixing_w, mixing_g, project_w, first, spread, second, act.at[m], after
         )
         for n in range(PAIR):
             mean_s[m, n : n + 1] = means[n]
@@ -464,7 +459,9 @@
         ],
         scratch_shapes=[
             pltpu.VMEM((OWN, 16, 64, 384), jnp.bfloat16),
+            pltpu.VMEM((PAIR, 16, GRID, GRID, C1), jnp.float32),
             pltpu.VMEM((PAIR, GRID, 64, 9 * C1), jnp.bfloat16),
+            pltpu.VMEM((PAIR, 512, C2), jnp.float32),
             pltpu.VMEM((STEPS, GRID, PAIR, 64, C2), jnp.bfloat16),
             pltpu.VMEM((STEPS, GRID, PAIR, 64, C2), jnp.bfloat16),
             near,

time: 120 us -> 120 us (level)
  no operation moved by 1% of the time
where the time goes in v5:
time: 120 us
  Pallas kernels  120 us (100%)
    pallas_call x1, Pallas kernels, exchange_call(): pl.pallas_call(exchange_kernel, in_specs=[scalar, anywhere] + [inside] *...  109 us
    pallas_call x1, Pallas kernels, decode_call(): pl.pallas_call(decode_kernel, in_specs=[pl.BlockSpec(memory_space=pltpu.S...  10.5 us

profile of v5, /device:TPU:1, one launch (start us, length us, event | category | flops | bytes accessed | tf_op | source)
XLA Modules:
  0.0 119.8 jit_solution(7531016492879950994)
XLA Ops:
  0.0 109.2 %exchange.1 = (bf16[2,4,4,8,64,256]{5,4,3,2,1,0:T(8,128)(2,1)}, f32[2,4,4,8,128]{4,3,2,1,0:T(8,128)}, s32[128]{0:T(128)}, s32[16,8,1,128]{3,2,1,0:T(1,128)}) custom-call(s32[1,8]{1,0:T(1,128)} %bitcast.13, bf16[8,16,64,384]{3,2,1,0:T(8,128)(2,1)} %pixels.1, bf16[384,128]{1,0:T(8,128)(2,1)} %embed_w.1, f32[1,128]{1,0:T(1,128)} %bitcast.14, ...), custom_call_target="tpu_custom_call" | custom-call | tf_op jit(solution)/shard_map/exchange/pallas_call | solution.py:450
  109.2 10.5 %decode.1 = bf16[256,64,512]{2,1,0:T(8,128)(2,1)} custom-call(s32[128]{0:T(128)} %get-tuple-element.8.state, bf16[2,16,8,64,256]{4,3,2,1,0:T(8,128)(2,1)} %bitcast.8, f32[2,16,8,128]{3,2,1,0:T(8,128)} %bitcast.10, bf16[256,512]{1,0:T(8,128)(2,1)} %weight.1, f32[1,512]{1,0:T(1,128)} %bitcast.11), custom_call_target="tpu_custom_call" | custom-call | tf_op jit(solution)/shard_map/decode/pallas_call | solution.py:566
